TPU v7x, 256 devices: a whole 4x4x8 slice. The times are simulated.
256 devices in a mesh: ctx: 32 (over z, x), ch: 8 (over y, core).
Axes of the slice: x: 4, y: 4, z: 8, core: 2. Of those that a mesh axis runs over, the one named last changes fastest.
Arguments:
- gate_q: bfloat16 [12288, 4096], P('ctx', 'ch'), may hold values from -6 to 6
- key_k: bfloat16 [12288, 4096], P('ctx', 'ch'), may hold values from -6 to 6
- value_v: bfloat16 [12288, 4096], P('ctx', 'ch'), may hold values from -6 to 6
- long_filter: bfloat16 [12288, 4096], P('ctx', 'ch'), may hold values from -0.0546875 to 0.0546875
- skip_gain: float32 [4096], P('ch'), may hold values from 0.5 to 1.5
- out_weight: bfloat16 [4096, 4096], P('ch'), may hold values from -0.125 to 0.125
Outputs:
- mixed: bfloat16 [12288, 4096], P('ctx', 'ch')
All inputs are finite; a program needn't handle non-finite values.
Results may differ from a plain program's by a relative error of at most 0.023.
Values may be sent and summed in bfloat16 or wider, within the bound.
A program may use at most 128 MiB of HBM per device.

v0:
```python
import math

import jax
import jax.numpy as jnp
from jax import lax
from jax.sharding import PartitionSpec as P


def for_sending(value):
    return jax.tree.map(lambda a: a.astype(jnp.bfloat16) if a.dtype == jnp.float32 else a, value)


def angle_table(left_index, right_index, length):
    turns = left_index[:, None] * right_index[None, :] % length
    angles = turns.astype(jnp.float32) * (2.0 * math.pi / length)
    return (jnp.cos(angles), jnp.sin(angles))


def local(gate_q, key_k, value_v, long_filter, skip_gain, out_weight):
    tok_rows, channels = key_k.shape
    group_count = lax.axis_size("ctx")
    position = lax.axis_index("ctx")
    block_rows = tok_rows // group_count
    full_len = 2 * group_count * tok_rows
    highest = lax.Precision.HIGHEST
    gated = (key_k.astype(jnp.float32) * value_v.astype(jnp.float32)).astype(jnp.bfloat16)
    freq_all = jnp.arange(2 * group_count, dtype=jnp.int32)
    block_index = jnp.arange(group_count, dtype=jnp.int32)
    row_index = jnp.arange(tok_rows, dtype=jnp.int32)
    cos_outer, sin_outer = angle_table(freq_all, block_index, 2 * group_count)
    cos_inner, sin_inner = angle_table(row_index, row_index, tok_rows)
    cos_final, sin_final = angle_table(block_index, freq_all, 2 * group_count)
    moved_gated, moved_filter = (
        lax.all_to_all(
            gated.reshape(group_count, block_rows, channels),
            "ctx",
            split_axis=0,
            concat_axis=0,
            tiled=True,
        ),
        lax.all_to_all(
            long_filter.reshape(group_count, block_rows, channels),
            "ctx",
            split_axis=0,
            concat_axis=0,
            tiled=True,
        ),
    )
    signals = jnp.stack([moved_gated, moved_filter]).astype(jnp.float32)
    outer_re = jnp.einsum("ka,sarc->skrc", cos_outer, signals, precision=highest)
    outer_im = -jnp.einsum("ka,sarc->skrc", sin_outer, signals, precision=highest)
    rows_here = position * block_rows + jnp.arange(block_rows, dtype=jnp.int32)
    twist_cos, twist_sin = angle_table(freq_all, rows_here, full_len)
    twist_cos = twist_cos[None, :, :, None]
    twist_sin = twist_sin[None, :, :, None]
    turned_re = outer_re * twist_cos + outer_im * twist_sin
    turned_im = outer_im * twist_cos - outer_re * twist_sin
    spectra = lax.all_to_all(
        jnp.stack([turned_re, turned_im], axis=1).astype(jnp.bfloat16),
        "ctx",
        split_axis=2,
        concat_axis=3,
        tiled=True,
    ).astype(jnp.float32)
    spec_re = jnp.einsum("kb,sebc->sekc", cos_inner, spectra[:, 0], precision=highest) + jnp.einsum(
        "kb,sebc->sekc", sin_inner, spectra[:, 1], precision=highest
    )
    spec_im = jnp.einsum("kb,sebc->sekc", cos_inner, spectra[:, 1], precision=highest) - jnp.einsum(
        "kb,sebc->sekc", sin_inner, spectra[:, 0], precision=highest
    )
    regrouped = lax.all_to_all(
        for_sending(jnp.stack([spec_re, spec_im])), "ctx", split_axis=3, concat_axis=2, tiled=True
    )
    ordered = jnp.swapaxes(regrouped, 2, 3)
    prod_re = ordered[0, 0] * ordered[0, 1] - ordered[1, 0] * ordered[1, 1]
    prod_im = ordered[0, 0] * ordered[1, 1] + ordered[1, 0] * ordered[0, 1]
    restored = lax.all_to_all(
        for_sending(jnp.swapaxes(jnp.stack([prod_re, prod_im]), 1, 2)),
        "ctx",
        split_axis=1,
        concat_axis=2,
        tiled=True,
    )
    prod_re = restored[0]
    prod_im = restored[1]
    back_re = jnp.einsum("bk,ekc->ebc", cos_inner, prod_re, precision=highest) - jnp.einsum(
        "bk,ekc->ebc", sin_inner, prod_im, precision=highest
    )
    back_im = jnp.einsum("bk,ekc->ebc", cos_inner, prod_im, precision=highest) + jnp.einsum(
        "bk,ekc->ebc", sin_inner, prod_re, precision=highest
    )
    own_freq = 2 * position + jnp.arange(2, dtype=jnp.int32)
    undo_cos, undo_sin = angle_table(own_freq, row_index, full_len)
    undo_cos = undo_cos[:, :, None]
    undo_sin = undo_sin[:, :, None]
    wound_re = back_re * undo_cos - back_im * undo_sin
    wound_im = back_im * undo_cos + back_re * undo_sin
    collected = lax.all_to_all(
        for_sending(jnp.stack([wound_re, wound_im])), "ctx", split_axis=2, concat_axis=1, tiled=True
    )
    finished = (
        jnp.einsum("ak,krc->arc", cos_final, collected[0], precision=highest)
        - jnp.einsum("ak,krc->arc", sin_final, collected[1], precision=highest)
    ) * (1.0 / full_len)
    arrived = lax.all_to_all(
        for_sending(finished), "ctx", split_axis=0, concat_axis=0, tiled=True
    ).astype(finished.dtype)
    conv = arrived.reshape(tok_rows, channels)
    hidden = (
        gate_q.astype(jnp.float32) * (conv + skip_gain[None, :] * gated.astype(jnp.float32))
    ).astype(jnp.bfloat16)
    terms = jnp.dot(hidden, out_weight, preferred_element_type=jnp.float32)
    return lax.psum_scatter(terms.astype(jnp.bfloat16), "ch", scatter_dimension=1, tiled=True)


def solution(mesh):
    placed = (
        P("ctx", "ch"),
        P("ctx", "ch"),
        P("ctx", "ch"),
        P("ctx", "ch"),
        P("ch"),
        P("ch", None),
    )
    return jax.shard_map(
        local, mesh=mesh, in_specs=placed, out_specs=P("ctx", "ch"), check_vma=False
    )
```

profile of v0, /device:TPU:1, one launch (start us, length us, event | category | flops | bytes accessed | tf_op | source)
XLA Modules:
  0.0 459.1 jit_solution(16877831459311176909)
XLA Ops:
  6.5 1.3 multiply_convert_fusion.1
  7.8 0.9 reshape.209
  8.7 11.9 %all-to-all-start = ((bf16[32,12,512]{2,1,0:T(8,128)(2,1)}), bf16[32,12,512]{2,1,0:T(8,128)(2,1)S(1)}, u32[]{:S(2)}, u32[]{:S(2)}) async-start(bf16[32,12,512]{2,1,0:T(8,128)(2,1)} %reshape.209), calls=%async_computation | async-start | bytes 1048576 | tf_op jit(solution)/shard_map/all_to_all | solution.py:34
  20.6 0.9 reshape.210
  21.4 15.4 %all-to-all-done = bf16[32,12,512]{2,1,0:T(8,128)(2,1)S(1)} async-done(((bf16[32,12,512]{2,1,0:T(8,128)(2,1)}), bf16[32,12,512]{2,1,0:T(8,128)(2,1)S(1)}, u32[]{:S(2)}, u32[]{:S(2)}) %all-to-all-start) | async-done | bytes 393248 | tf_op jit(solution)/shard_map/all_to_all | solution.py:34
  36.8 5.2 %all-to-all-start.1 = ((bf16[32,12,512]{2,1,0:T(8,128)(2,1)}), bf16[32,12,512]{2,1,0:T(8,128)(2,1)S(1)}, u32[]{:S(2)}, u32[]{:S(2)}) async-start(bf16[32,12,512]{2,1,0:T(8,128)(2,1)} %reshape.210), calls=%async_computation.1 | async-start | bytes 1048576 | tf_op jit(solution)/shard_map/all_to_all | solution.py:41
  42.1 0.1 fusion.100
  42.2 0.2 copy.133
  42.4 14.7 %all-to-all-done.1 = bf16[32,12,512]{2,1,0:T(8,128)(2,1)S(1)} async-done(((bf16[32,12,512]{2,1,0:T(8,128)(2,1)}), bf16[32,12,512]{2,1,0:T(8,128)(2,1)S(1)}, u32[]{:S(2)}, u32[]{:S(2)}) %all-to-all-start.1) | async-done | bytes 393248 | tf_op jit(solution)/shard_map/all_to_all | solution.py:41
  57.1 0.2 copy.132
  57.3 1.8 fusion.47
  59.1 2.8 fusion.5
  61.9 0.3 pad_maximum_fusion
  62.2 3.2 copy.100
  65.5 77.0 %all_to_all.81 = bf16[2,2,64,12,512]{4,1,3,0,2:T(2,128)(2,1)S(1)} all-to-all(bf16[2,2,64,12,512]{4,1,3,0,2:T(2,128)(2,1)S(1)} %copy.100), channel_id=1, replica_groups=mesh['ctx'=32,'ch'=8] {'ctx'}, dimensions={2} | all-to-all | bytes 6291456 | tf_op jit(solution)/shard_map/all_to_all | solution.py:58
  142.4 3.2 copy.101
  145.6 3.1 fusion.152
  148.7 1.4 copy.126
  150.1 6.6 %fusion.10 = f32[2,2,512,384]{3,2,1,0:T(8,128)} fusion(bf16[2,1,2,384,512]{3,4,2,0,1:T(8,128)(2,1)S(1)} %copy.126), kind=kOutput, calls=%fused_computation.21 | convolution fusion | flops 3625205760 | bytes 4718592 | tf_op jit(solution)/shard_map/kb,sebc->sekc/dot_general | solution.py:65
  156.7 3.9 copy.127
  160.6 0.0 copy-start
  160.6 5.1 %fusion.6 = f32[2,2,512,384]{3,2,1,0:T(8,128)S(1)} fusion(bf16[2,1,2,384,512]{3,4,2,0,1:T(8,128)(2,1)S(1)} %copy.127), kind=kOutput, calls=%fused_computation.17 | convolution fusion | flops 3625205760 | bytes 4718592 | tf_op jit(solution)/shard_map/kb,sebc->sekc/dot_general | solution.py:68
  165.8 4.9 %fusion.12 = bf16[1,2,2,384,512]{3,4,2,1,0:T(8,128)(2,1)S(1)} fusion(f32[2,2,512,384]{3,2,1,0:T(8,128)S(1)} %copy-done, bf16[2,1,2,384,512]{3,4,2,0,1:T(8,128)(2,1)S(1)} %copy.127), kind=kOutput, calls=%fused_computation.27 | convolution fusion | flops 3626778624 | bytes 6291456 | tf_op jit(solution)/shard_map/kb,sebc->sekc/dot_general | solution.py:65
  170.7 5.3 %fusion.15 = bf16[1,2,2,384,512]{3,4,2,1,0:T(8,128)(2,1)S(1)} fusion(f32[2,2,512,384]{3,2,1,0:T(8,128)S(1)} %fusion.6, bf16[2,1,2,384,512]{3,4,2,0,1:T(8,128)(2,1)S(1)} %copy.126), kind=kOutput, calls=%fused_computation.28 | convolution fusion | flops 3626778624 | bytes 6291456 | tf_op jit(solution)/shard_map/kb,sebc->sekc/dot_general | solution.py:68
  176.0 0.4 pad_maximum_fusion.1
  176.4 6.0 %copy.104 = bf16[2,2,2,384,512]{4,2,1,0,3:T(2,128)(2,1)} copy(bf16[2,2,2,384,512]{3,4,2,1,0:T(8,128)(2,1)S(1)} %pad_maximum_fusion.1) | data formatting | bytes 6291456 | tf_op jit(solution)/shard_map/stack | solution.py:72
  182.5 76.2 %all_to_all.82 = bf16[2,2,2,384,512]{4,2,1,0,3:T(2,128)(2,1)S(1)} all-to-all(bf16[2,2,2,384,512]{4,2,1,0,3:T(2,128)(2,1)} %copy.104), channel_id=1, replica_groups=mesh['ctx'=32,'ch'=8] {'ctx'}, dimensions={3} | all-to-all | bytes 6291456 | tf_op jit(solution)/shard_map/all_to_all | solution.py:71
  258.7 3.5 copy.106
  262.2 6.1 %multiply_subtract_fusion = (bf16[1,1,12,64,512]{4,1,2,3,0:T(2,128)(2,1)S(1)}, bf16[1,1,12,64,512]{4,1,2,3,0:T(2,128)(2,1)S(1)}) fusion(bf16[2,2,12,64,512]{4,1,2,3,0:T(2,128)(2,1)S(1)} %bitcast.145), kind=kLoop, calls=%fused_computation.26 | loop fusion | flops 2359296 | bytes 4718592 | tf_op jit(solution)/shard_map/sub | solution.py:75
  268.4 0.9 copy_bitcast_fusion
  269.3 0.1 maximum_bitcast_fusion
  269.4 2.8 copy.109
  272.2 7.4 %all-to-all-start.4 = ((bf16[2,64,12,512]{3,0,2,1:T(2,128)(2,1)}), bf16[2,64,12,512]{3,0,2,1:T(2,128)(2,1)S(1)}, u32[]{:S(2)}, u32[]{:S(2)}) async-start(bf16[2,64,12,512]{3,0,2,1:T(2,128)(2,1)} %copy.109), calls=%async_computation.4 | async-start | bytes 3145728 | tf_op jit(solution)/shard_map/all_to_all | solution.py:77
  279.6 0.4 reduce-scatter.2.cloned.1.call-start
  280.1 0.1 fusion.109
  280.2 34.6 %all-to-all-done.4 = bf16[2,64,12,512]{3,0,2,1:T(2,128)(2,1)S(1)} async-done(((bf16[2,64,12,512]{3,0,2,1:T(2,128)(2,1)}), bf16[2,64,12,512]{3,0,2,1:T(2,128)(2,1)S(1)}, u32[]{:S(2)}, u32[]{:S(2)}) %all-to-all-start.4) | async-done | bytes 1572896 | tf_op jit(solution)/shard_map/all_to_all | solution.py:77
  314.9 3.6 fusion.154
  318.5 0.8 copy.112
  319.3 0.7 copy.113
  320.0 4.9 %fusion.26 = f32[2,512,384]{2,1,0:T(8,128)} fusion(bf16[2,384,512]{1,2,0:T(8,128)(2,1)S(1)} %copy.113), kind=kOutput, calls=%fused_computation.46 | convolution fusion | flops 1813266432 | bytes 2359296 | tf_op jit(solution)/shard_map/bk,ekc->ebc/dot_general | solution.py:89
  324.9 0.8 copy.110
  325.7 0.9 copy.111
  326.6 3.7 fusion.28
  330.4 3.7 convolution_add_fusion
  334.1 4.8 %fusion.20 = (bf16[1,2,384,512]{2,3,1,0:T(8,128)(2,1)S(1)}, bf16[1,2,384,512]{2,3,1,0:T(8,128)(2,1)S(1)}) fusion(f32[2,512,384]{2,1,0:T(8,128)S(1)} %convolution_add_fusion, f32[2,384]{1,0:T(2,128)S(1)} %get-tuple-element.18, f32[2,384]{1,0:T(2,128)S(1)} %get-tuple-element.17, f32[2,512,384]{2,1,0:T(8,128)S(1)} %fusion.28, bf16[2,384,512]{1,2,0:T(8,128)(2,1)S(1)} %copy.113), kind=kOutput, calls=%fused_computation.35 | convolution fusion | flops 1816805376 | bytes 5511168 | tf_op jit(solution)/shard_map/bk,ekc->ebc/dot_general | solution.py:86
  338.9 0.2 pad_maximum_fusion.2
  339.1 1.6 copy.116
  340.7 43.4 %all_to_all.83 = bf16[2,2,384,512]{3,1,0,2:T(2,128)(2,1)S(1)} all-to-all(bf16[2,2,384,512]{3,1,0,2:T(2,128)(2,1)S(1)} %copy.116), channel_id=1, replica_groups=mesh['ctx'=32,'ch'=8] {'ctx'}, dimensions={2} | all-to-all | bytes 3145728 | tf_op jit(solution)/shard_map/all_to_all | solution.py:98
  384.1 1.1 copy.117
  385.2 1.1 fusion.153
  386.3 0.7 copy.118
  387.0 0.3 squeeze.32
  387.3 0.5 fusion.83
  387.8 0.7 copy.119
  388.5 0.3 squeeze.33
  388.8 0.5 fusion.19
  389.4 0.0 copy-start.3
  389.4 0.0 copy-start.4
  389.4 0.2 copy.120
  389.6 20.0 %all_to_all.84 = bf16[32,12,512]{2,1,0:T(8,128)(2,1)S(1)} all-to-all(bf16[32,12,512]{2,1,0:T(8,128)(2,1)S(1)} %copy.120), channel_id=1, replica_groups=mesh['ctx'=32,'ch'=8] {'ctx'}, dimensions={0} | all-to-all | bytes 786432 | tf_op jit(solution)/shard_map/all_to_all | solution.py:105
  409.7 0.1 reshape.214
  409.8 5.7 %convolution_convert_fusion = bf16[384,4096]{1,0:T(8,128)(2,1)} fusion(bf16[512,4096]{1,0:T(8,128)(2,1)} %param.11, f32[384,512]{1,0:T(8,128)S(1)} %reshape.214, bf16[384,512]{1,0:T(8,128)(2,1)S(1)} %multiply_convert_fusion.1, bf16[384,512]{1,0:T(8,128)(2,1)S(1)} %copy-done.3, f32[512]{0:T(512)S(1)} %copy-done.4), kind=kOutput, calls=%fused_computation | convolution fusion | flops 1613365248 | bytes 8914944 | tf_op jit(solution)/shard_map/dot_general | solution.py:112
  415.4 0.0 reduce-scatter.2.cloned.1.call-update
  415.5 36.6 %reduce-scatter.2.cloned.1.call-done = bf16[384,512]{1,0:T(8,128)(2,1)} async-done(((bf16[384,4096]{1,0:T(8,128)(2,1)}), bf16[384,512]{1,0:T(8,128)(2,1)}) %reduce-scatter.2.cloned.1.call-update) | async-done | bytes 393232 | tf_op jit(solution)/shard_map/reduce_scatter | solution.py:113
  (9 shorter events, 0.0 us)
Async XLA Ops:
  6.5 14.0 %copy-start.2 = (bf16[384,512]{1,0:T(8,128)(2,1)S(1)}, bf16[384,512]{1,0:T(8,128)(2,1)}, u32[]{:S(2)}) copy-start(bf16[384,512]{1,0:T(8,128)(2,1)} %param.9) | copy-start | bytes 1179652
  8.7 28.1 %all-to-all-start = ((bf16[32,12,512]{2,1,0:T(8,128)(2,1)}), bf16[32,12,512]{2,1,0:T(8,128)(2,1)S(1)}, u32[]{:S(2)}, u32[]{:S(2)}) async-start(bf16[32,12,512]{2,1,0:T(8,128)(2,1)} %reshape.209), calls=%async_computation | async-start | bytes 1048576 | tf_op jit(solution)/shard_map/all_to_all | solution.py:34
  36.8 20.3 %all-to-all-start.1 = ((bf16[32,12,512]{2,1,0:T(8,128)(2,1)}), bf16[32,12,512]{2,1,0:T(8,128)(2,1)S(1)}, u32[]{:S(2)}, u32[]{:S(2)}) async-start(bf16[32,12,512]{2,1,0:T(8,128)(2,1)} %reshape.210), calls=%async_computation.1 | async-start | bytes 1048576 | tf_op jit(solution)/shard_map/all_to_all | solution.py:41
  160.6 5.2 %copy-start = (f32[2,2,512,384]{3,2,1,0:T(8,128)S(1)}, f32[2,2,512,384]{3,2,1,0:T(8,128)}, u32[]{:S(2)}) copy-start(f32[2,2,512,384]{3,2,1,0:T(8,128)} %fusion.10) | copy-start | bytes 9437188
  272.2 42.7 %all-to-all-start.4 = ((bf16[2,64,12,512]{3,0,2,1:T(2,128)(2,1)}), bf16[2,64,12,512]{3,0,2,1:T(2,128)(2,1)S(1)}, u32[]{:S(2)}, u32[]{:S(2)}) async-start(bf16[2,64,12,512]{3,0,2,1:T(2,128)(2,1)} %copy.109), calls=%async_computation.4 | async-start | bytes 3145728 | tf_op jit(solution)/shard_map/all_to_all | solution.py:77
  279.6 172.4 %reduce-scatter.2.cloned.1.call-start = ((), (), s32[]{:S(2)}) async-start(), calls=%async_computation.8 | async-start | bytes 3538944 | tf_op jit(solution)/shard_map/reduce_scatter | solution.py:113
  326.6 3.7 copy-start.1
  389.4 20.4 %copy-start.3 = (bf16[384,512]{1,0:T(8,128)(2,1)S(1)}, bf16[384,512]{1,0:T(8,128)(2,1)}, u32[]{:S(2)}) copy-start(bf16[384,512]{1,0:T(8,128)(2,1)} %param.6) | copy-start | bytes 1179652
  389.4 20.4 %copy-start.4 = (f32[512]{0:T(512)S(1)}, f32[512]{0:T(512)}, u32[]{:S(2)}) copy-start(f32[512]{0:T(512)} %param.10) | copy-start | bytes 6148
Sparse Core Ops, SparseCore 0:
  415.6 36.4 reduce-scatter.1
where the time goes:
time: 468 us; the launch traced here: 459 us
  blocking collectives  217 us (46%)
  waiting for transfers between devices  101 us (22%)
  matrix products  50.4 us (11%)
  local copies, waits for them, and re-layouts  43.2 us (9%)
  starting transfers between devices  24.9 us (5%)
  between operations  14 us (3%)
  other arithmetic  8.66 us (2%)
    all_to_all x1, blocking collectives, local(): lax.all_to_all(jnp.stack([turned_re, turned_im], axis=1).astype(jnp.bfloa...  77 us
    all_to_all x1, blocking collectives, local(): lax.all_to_all(for_sending(jnp.stack([spec_re, spec_im])), 'ctx', split_a...  76.2 us
    all_to_all x1, blocking collectives, local(): lax.all_to_all(for_sending(jnp.stack([wound_re, wound_im])), 'ctx', split...  43.4 us
    reduce_scatter x1, waiting for transfers between devices, local(): lax.psum_scatter(terms.astype(jnp.bfloat16), 'ch', scatter_dimension=1, t...  36.6 us
    all_to_all x1, waiting for transfers between devices, local(): lax.all_to_all(for_sending(jnp.swapaxes(jnp.stack([prod_re, prod_im]), 1,...  34.6 us
    all_to_all x1, blocking collectives, local(): lax.all_to_all(for_sending(finished), 'ctx', split_axis=0, concat_axis=0,...  20 us
    all_to_all x1, waiting for transfers between devices, local(): lax.all_to_all(gated.reshape(group_count, block_rows, channels), 'ctx', s...  15.4 us
    all_to_all x1, waiting for transfers between devices, local(): lax.all_to_all(long_filter.reshape(group_count, block_rows, channels), 'c...  14.7 us
  transfers between devices with their start and end apart: 4, of which 4 were waited for; matrix products, arithmetic and copies ran while one was open for 0% of the time, Pallas kernels for 0%

commit v1 on v0

v1 whole, which is shorter than its diff:
```python
import jax
import jax.numpy as jnp
import numpy as np
from jax import lax
from jax.sharding import PartitionSpec as P


def tables(blocks, rows):
    half = np.arange(blocks) + 0.5
    outer = 2.0 * np.pi * np.outer(half, np.arange(blocks)) / (2 * blocks)
    twist = 2.0 * np.pi * np.outer(half, np.arange(rows)) / (2 * blocks * rows)
    inner = 2.0 * np.pi * (np.outer(np.arange(rows), np.arange(rows)) % rows) / rows
    return outer, twist, inner


def local(gate_q, key_k, value_v, long_filter, skip_gain, out_weight):
    rows, channels = key_k.shape
    blocks = lax.axis_size("ctx")
    own = channels // blocks
    outer, twist, inner = tables(blocks, rows)
    outer_cos = jnp.asarray(np.cos(outer), jnp.bfloat16)
    outer_sin = jnp.asarray(-np.sin(outer), jnp.bfloat16)
    twist_cos = jnp.asarray(np.cos(twist), jnp.float32)[:, None, :]
    twist_sin = jnp.asarray(np.sin(twist), jnp.float32)[:, None, :]
    cos, sin = np.cos(inner), np.sin(inner)
    ahead = jnp.asarray(np.block([[cos, -sin], [sin, cos]]), jnp.bfloat16)

    gated = (key_k.astype(jnp.float32) * value_v.astype(jnp.float32)).astype(jnp.bfloat16)

    def exchange(value):
        return lax.all_to_all(
            value.reshape(blocks, own, rows), "ctx", split_axis=0, concat_axis=0, tiled=True
        )

    def spectrum(signal):
        re = jnp.einsum("kn,ncp->kcp", outer_cos, signal, preferred_element_type=jnp.float32)
        im = jnp.einsum("kn,ncp->kcp", outer_sin, signal, preferred_element_type=jnp.float32)
        turned = jnp.concatenate(
            [re * twist_cos + im * twist_sin, im * twist_cos - re * twist_sin], axis=2
        ).astype(jnp.bfloat16)
        return jnp.einsum("kcp,pf->kcf", turned, ahead, preferred_element_type=jnp.float32)

    filter_spec = spectrum(exchange(long_filter.T))
    gated_spec = spectrum(exchange(gated.T))
    fr, fi = filter_spec[..., :rows], filter_spec[..., rows:]
    gr, gi = gated_spec[..., :rows], gated_spec[..., rows:]
    product = jnp.concatenate([fr * gr - fi * gi, fr * gi + fi * gr], axis=2).astype(jnp.bfloat16)
    back = jnp.einsum("kcf,pf->kcp", product, ahead, preferred_element_type=jnp.float32)
    br, bi = back[..., :rows], back[..., rows:]
    wound_re = (br * twist_cos - bi * twist_sin).astype(jnp.bfloat16)
    wound_im = (bi * twist_cos + br * twist_sin).astype(jnp.bfloat16)
    finished = jnp.einsum(
        "kn,kcp->ncp", outer_cos, wound_re, preferred_element_type=jnp.float32
    ) + jnp.einsum("kn,kcp->ncp", outer_sin, wound_im, preferred_element_type=jnp.float32)
    finished = (finished * (1.0 / (blocks * rows))).astype(jnp.bfloat16)
    arrived = lax.all_to_all(finished, "ctx", split_axis=0, concat_axis=0, tiled=True)
    conv = arrived.reshape(channels, rows).T.astype(jnp.float32)
    hidden = (
        gate_q.astype(jnp.float32) * (conv + skip_gain[None, :] * gated.astype(jnp.float32))
    ).astype(jnp.bfloat16)
    terms = jnp.dot(hidden, out_weight, preferred_element_type=jnp.float32)
    return lax.psum_scatter(terms.astype(jnp.bfloat16), "ch", scatter_dimension=1, tiled=True)


def solution(mesh):
    placed = (
        P("ctx", "ch"),
        P("ctx", "ch"),
        P("ctx", "ch"),
        P("ctx", "ch"),
        P("ch"),
        P("ch", None),
    )
    return jax.shard_map(
        local, mesh=mesh, in_specs=placed, out_specs=P("ctx", "ch"), check_vma=False
    )
```

time: 468 us -> 128 us (0.27); the launches traced: 459 us -> 126 us
  blocking collectives: 217 us -> 0 us
  matrix products: 50.4 us -> 10.9 us
  local copies, waits for them, and re-layouts: 43.2 us -> 5.57 us
  waiting for transfers between devices: 101 us -> 72.1 us
  other arithmetic: 8.66 us -> 1.38 us
    all_to_all x4 -> x0, blocking collectives: 217 us -> none  [the longest x1 77 us: local(): lax.all_to_all(jnp.stack([turned_re, turned_im], axis=1).astype(jnp.bfloa...]
    dot_general x12 -> x9, matrix products: 44.7 us -> 4.97 us  [the longest x2 2.2 us: spectrum(): jnp.einsum('kcp,pf->kcf', turned, ahead, preferred_element_type=jnp.float32)]
    all_to_all x3, waiting for transfers between devices: 64.7 us -> 37.5 us  [the longest x2 25.2 us: exchange(): lax.all_to_all(value.reshape(blocks, own, rows), 'ctx', split_axis=0, con...]
    another operation x3 -> x0, local copies, waits for them, and re-layouts: 10.9 us -> none  [the longest x1 6.05 us: local(): jnp.stack([spec_re, spec_im])]
    slice x7 -> x0, local copies, waits for them, and re-layouts: 10.7 us -> none  [the longest x2 4.42 us: local(): prod_im = restored[1]]
    all_to_all x5 -> x0, local copies, waits for them, and re-layouts: 8.3 us -> none  [the longest x1 3.54 us: local(): lax.all_to_all(for_sending(jnp.stack([spec_re, spec_im])), 'ctx', split_a...]
    sub x1 -> x0, other arithmetic: 6.15 us -> none  [local(): prod_re = ordered[0, 0] * ordered[0, 1] - ordered[1, 0] * ordered[1, 1]]
  transfers between devices with their start and end apart: 4 -> 4, of which waited for: 4 -> 4; matrix products, arithmetic and copies ran while one was open for 0% -> 1% of each run, Pallas kernels for 0% -> 0%
where the time goes in v1:
time: 128 us; the launch traced here: 126 us
  waiting for transfers between devices  72.1 us (56%)
  starting transfers between devices  22.5 us (18%)
  between operations  13.6 us (11%)
  matrix products  10.9 us (9%)
  local copies, waits for them, and re-layouts  5.57 us (4%)
  other arithmetic  1.38 us (1%)
    reduce_scatter x1, waiting for transfers between devices, local(): lax.psum_scatter(terms.astype(jnp.bfloat16), 'ch', scatter_dimension=1, t...  34.6 us
    all_to_all x2, waiting for transfers between devices, exchange(): lax.all_to_all(value.reshape(blocks, own, rows), 'ctx', split_axis=0, con...  25.2 us
    all_to_all x2, starting transfers between devices, exchange(): lax.all_to_all(value.reshape(blocks, own, rows), 'ctx', split_axis=0, con...  16.9 us
    all_to_all x1, waiting for transfers between devices, local(): lax.all_to_all(finished, 'ctx', split_axis=0, concat_axis=0, tiled=True)  12.3 us
    dot_general x1, matrix products, local(): terms = jnp.dot(hidden, out_weight, preferred_element_type=jnp.float32)  5.91 us
    all_to_all x1, starting transfers between devices, local(): lax.all_to_all(finished, 'ctx', split_axis=0, concat_axis=0, tiled=True)  5.64 us
    unnamed x20, local copies, waits for them, and re-layouts  4.69 us
  transfers between devices with their start and end apart: 4, of which 4 were waited for; matrix products, arithmetic and copies ran while one was open for 1% of the time, Pallas kernels for 0%

profile of v1, /device:TPU:1, one launch (start us, length us, event | category | flops | bytes accessed | tf_op | source)
XLA Modules:
  0.0 126.1 jit_solution(809013198664377853)
XLA Ops:
  6.5 1.2 copy.36
  7.7 0.0 copy-start.2
  7.8 1.3 copy.37
  9.0 0.0 copy-start.4
  9.0 0.9 multiply_convert_fusion
  9.9 11.9 %all-to-all-start.1 = ((bf16[32,16,384]{2,1,0:T(8,128)(2,1)}), bf16[32,16,384]{2,1,0:T(8,128)(2,1)S(1)}, u32[]{:S(2)}, u32[]{:S(2)}) async-start(bf16[32,16,384]{2,1,0:T(8,128)(2,1)} %bitcast.6), calls=%async_computation.1 | async-start | bytes 786432 | tf_op jit(solution)/shard_map/all_to_all | solution.py:31
  21.8 0.0 copy-done.2
  21.8 0.0 copy-start.5
  21.8 0.9 copy.32
  22.7 12.9 %all-to-all-done.1 = bf16[32,16,384]{2,1,0:T(8,128)(2,1)S(1)} async-done(((bf16[32,16,384]{2,1,0:T(8,128)(2,1)}), bf16[32,16,384]{2,1,0:T(8,128)(2,1)S(1)}, u32[]{:S(2)}, u32[]{:S(2)}) %all-to-all-start.1) | async-done | bytes 393248 | tf_op jit(solution)/shard_map/all_to_all | solution.py:31
  35.6 5.0 %all-to-all-start = ((bf16[32,16,384]{2,1,0:T(8,128)(2,1)}), bf16[32,16,384]{2,1,0:T(8,128)(2,1)S(1)}, u32[]{:S(2)}, u32[]{:S(2)}) async-start(bf16[32,16,384]{2,1,0:T(8,128)(2,1)} %bitcast.2), calls=%async_computation | async-start | bytes 786432 | tf_op jit(solution)/shard_map/all_to_all | solution.py:31
  40.6 0.0 copy-done.4
  40.6 0.0 copy-start
  40.6 0.0 copy-start.1
  40.6 0.2 fusion.19
  40.9 0.0 copy-done.5
  40.9 0.3 fusion.21
  41.1 12.3 %all-to-all-done = bf16[32,16,384]{2,1,0:T(8,128)(2,1)S(1)} async-done(((bf16[32,16,384]{2,1,0:T(8,128)(2,1)}), bf16[32,16,384]{2,1,0:T(8,128)(2,1)S(1)}, u32[]{:S(2)}, u32[]{:S(2)}) %all-to-all-start) | async-done | bytes 393248 | tf_op jit(solution)/shard_map/all_to_all | solution.py:31
  53.5 0.2 fusion.25
  53.7 0.0 copy-done
  53.7 0.0 copy-done.1
  53.7 0.5 add_convert_fusion.3
  54.2 0.0 copy-start.7
  54.2 0.2 pad_maximum_fusion
  54.5 1.0 copy-done.7
  55.5 1.1 fusion.10
  56.6 1.1 fusion.8
  57.7 0.3 subtract_convert_fusion.1
  58.0 0.1 pad_maximum_fusion.2
  58.1 0.9 fusion.6
  59.0 0.3 fusion.12
  59.3 0.0 copy-start.3
  59.3 0.3 fusion.2
  59.6 0.0 copy-start.6
  59.6 0.9 copy.45
  60.5 5.6 %all-to-all-start.2 = ((bf16[32,16,384]{2,1,0:T(8,128)(2,1)}), bf16[32,16,384]{2,1,0:T(8,128)(2,1)S(1)}, u32[]{:S(2)}, u32[]{:S(2)}) async-start(bf16[32,16,384]{2,1,0:T(8,128)(2,1)} %copy.45), calls=%async_computation.2 | async-start | bytes 786432 | tf_op jit(solution)/shard_map/all_to_all | solution.py:56
  66.2 0.0 reduce-scatter.2.cloned.1.call-start
  66.2 0.0 copy-done.3
  66.2 0.2 copy.31
  66.4 12.3 %all-to-all-done.2 = bf16[32,16,384]{2,1,0:T(8,128)(2,1)S(1)} async-done(((bf16[32,16,384]{2,1,0:T(8,128)(2,1)}), bf16[32,16,384]{2,1,0:T(8,128)(2,1)S(1)}, u32[]{:S(2)}, u32[]{:S(2)}) %all-to-all-start.2) | async-done | bytes 393248 | tf_op jit(solution)/shard_map/all_to_all | solution.py:56
  78.7 0.0 copy-done.6
  78.7 5.9 %convolution_convert_fusion = bf16[384,4096]{1,0:T(8,128)(2,1)} fusion(bf16[512,4096]{1,0:T(8,128)(2,1)} %param.16, bf16[512,384]{1,0:T(8,128)(2,1)S(1)} %bitcast.34, bf16[384,512]{0,1:T(8,128)(2,1)} %multiply_convert_fusion, bf16[384,512]{0,1:T(8,128)(2,1)S(1)} %copy.31, f32[512]{0:T(512)S(1)} %copy-done.6), kind=kOutput, calls=%fused_computation | convolution fusion | flops 1613561856 | bytes 8521728 | tf_op jit(solution)/shard_map/dot_general | solution.py:61
  84.6 0.0 reduce-scatter.2.cloned.1.call-update
  84.7 34.6 %reduce-scatter.2.cloned.1.call-done = bf16[384,512]{1,0:T(8,128)(2,1)} async-done(((bf16[384,4096]{1,0:T(8,128)(2,1)}), bf16[384,512]{1,0:T(8,128)(2,1)}) %reduce-scatter.2.cloned.1.call-update) | async-done | bytes 393232 | tf_op jit(solution)/shard_map/reduce_scatter | solution.py:62
Async XLA Ops:
  7.7 14.0 %copy-start.2 = (bf16[384,512]{1,0:T(8,128)(2,1)S(1)}, bf16[384,512]{1,0:T(8,128)(2,1)}, u32[]{:S(2)}) copy-start(bf16[384,512]{1,0:T(8,128)(2,1)} %param.14) | copy-start | bytes 1179652
  9.0 31.6 %copy-start.4 = (bf16[32,32,1]{1,0,2:T(8,128)(2,1)S(1)}, bf16[32,32,1]{1,0,2:T(8,128)(2,1)}, u32[]{:S(2)}) copy-start(bf16[32,32,1]{1,0,2:T(8,128)(2,1)} %constant.18) | copy-start | bytes 6148
  9.9 25.7 %all-to-all-start.1 = ((bf16[32,16,384]{2,1,0:T(8,128)(2,1)}), bf16[32,16,384]{2,1,0:T(8,128)(2,1)S(1)}, u32[]{:S(2)}, u32[]{:S(2)}) async-start(bf16[32,16,384]{2,1,0:T(8,128)(2,1)} %bitcast.6), calls=%async_computation.1 | async-start | bytes 786432 | tf_op jit(solution)/shard_map/all_to_all | solution.py:31
  21.8 19.1 %copy-start.5 = (bf16[32,32,1]{1,0,2:T(8,128)(2,1)S(1)}, bf16[32,32,1]{1,0,2:T(8,128)(2,1)}, u32[]{:S(2)}) copy-start(bf16[32,32,1]{1,0,2:T(8,128)(2,1)} %constant.17) | copy-start | bytes 6148
  35.6 17.9 %all-to-all-start = ((bf16[32,16,384]{2,1,0:T(8,128)(2,1)}), bf16[32,16,384]{2,1,0:T(8,128)(2,1)S(1)}, u32[]{:S(2)}, u32[]{:S(2)}) async-start(bf16[32,16,384]{2,1,0:T(8,128)(2,1)} %bitcast.2), calls=%async_computation | async-start | bytes 786432 | tf_op jit(solution)/shard_map/all_to_all | solution.py:31
  40.6 13.1 %copy-start = (f32[32,384]{1,0:T(8,128)S(1)}, f32[32,384]{1,0:T(8,128)}, u32[]{:S(2)}) copy-start(f32[32,384]{1,0:T(8,128)} %constant.14.clone) | copy-start | bytes 147460
  40.6 13.1 %copy-start.1 = (f32[32,384]{1,0:T(8,128)S(1)}, f32[32,384]{1,0:T(8,128)}, u32[]{:S(2)}) copy-start(f32[32,384]{1,0:T(8,128)} %constant.15.clone) | copy-start | bytes 147460
  54.2 1.3 %copy-start.7 = (bf16[768,768,1]{1,0,2:T(8,128)(2,1)S(1)}, bf16[768,768,1]{1,0,2:T(8,128)(2,1)}, u32[]{:S(2)}) copy-start(bf16[768,768,1]{1,0,2:T(8,128)(2,1)} %constant.19) | copy-start | bytes 3538948
  59.3 6.9 %copy-start.3 = (bf16[384,512]{1,0:T(8,128)(2,1)S(1)}, bf16[384,512]{1,0:T(8,128)(2,1)}, u32[]{:S(2)}) copy-start(bf16[384,512]{1,0:T(8,128)(2,1)} %param.11) | copy-start | bytes 1179652
  59.6 19.1 %copy-start.6 = (f32[512]{0:T(512)S(1)}, f32[512]{0:T(512)}, u32[]{:S(2)}) copy-start(f32[512]{0:T(512)} %param.15) | copy-start | bytes 6148
  60.5 18.2 %all-to-all-start.2 = ((bf16[32,16,384]{2,1,0:T(8,128)(2,1)}), bf16[32,16,384]{2,1,0:T(8,128)(2,1)S(1)}, u32[]{:S(2)}, u32[]{:S(2)}) async-start(bf16[32,16,384]{2,1,0:T(8,128)(2,1)} %copy.45), calls=%async_computation.2 | async-start | bytes 786432 | tf_op jit(solution)/shard_map/all_to_all | solution.py:56
  66.2 53.1 %reduce-scatter.2.cloned.1.call-start = ((), (), s32[]{:S(2)}) async-start(), calls=%async_computation.4 | async-start | bytes 3538944 | tf_op jit(solution)/shard_map/reduce_scatter | solution.py:62
Sparse Core Ops, SparseCore 0:
  84.8 34.4 reduce-scatter.1

commit v2 on v1

v2 whole, which is shorter than its diff:
```python
import functools

import jax
import jax.numpy as jnp
import numpy as np
from jax import lax
from jax.experimental import pallas as pl
from jax.experimental.pallas import tpu as pltpu
from jax.sharding import PartitionSpec as P

MESH = pl.DeviceIdType.MESH
F32 = jnp.float32
BF16 = jnp.bfloat16
PARTS = 3


def tables(blocks, own, rows):
    half = np.arange(blocks) + 0.5
    outer = 2.0 * np.pi * np.outer(half, np.arange(blocks)) / (2 * blocks)
    twist = 2.0 * np.pi * np.outer(half, np.arange(rows)) / (2 * blocks * rows)
    inner = 2.0 * np.pi * (np.outer(np.arange(rows), np.arange(rows)) % rows) / rows
    wide = np.stack(
        [
            np.repeat(np.cos(outer), own, axis=1),
            np.repeat(-np.sin(outer), own, axis=1),
            np.repeat(np.cos(outer).T, own, axis=1),
            np.repeat(-np.sin(outer).T, own, axis=1),
        ]
    )
    turn = np.stack([np.cos(twist), np.sin(twist)])
    cos, sin = np.cos(inner), np.sin(inner)
    ahead = np.block([[cos, -sin], [sin, cos]])
    return jnp.asarray(wide, F32), jnp.asarray(turn, F32), jnp.asarray(ahead, BF16)


def dot(a, b):
    return jnp.dot(a, b, preferred_element_type=F32)


def far_first(step, count):
    half = (step + 1) // 2
    return (count // 2 + half * (1 - 2 * (step % 2))) % count


def kernel(
    dims,
    q_hbm, k_hbm, v_hbm, f_hbm, skip_ref, w_hbm, wide_ref, turn_ref, ahead_hbm,
    out_ref,
    qb, kb, vb, fb, gated, send_f, send_g, recv_f, recv_g, ahead, kron_f, kron_i, tcos, tsin,
    spec, wound, send_y, recv_y, hid, wx, p_own, p_up, p_down, send_a, recv_a, send_n, recv_n,
    lsem, wl_sem, ws_sem, wr_sem, fs_sem, fr_sem, gs_sem, gr_sem, ys_sem, yr_sem,
    hs_sem, hr_sem, as_sem, ar_sem, ns_sem, nr_sem,
):
    blocks, nx, own, rows, chips = dims
    nz = blocks // nx
    channels = blocks * own
    part = rows // PARTS
    cols = wx.shape[3]
    me = lax.axis_index("ctx")
    mz, mx = me // nx, me % nx
    cj = lax.axis_index("ch")
    y, core = cj // 2, cj % 2
    partner = cj + 1 - 2 * core
    y_up, y_far, y_down = (y + 1) % chips, (y + 2) % chips, (y + 3) % chips
    up, down = y_up * 2 + core, y_down * 2 + core

    def peer(step):
        z = (mz + far_first(step // nx, nz)) % nz
        x = (mx + far_first(step % nx, nx)) % nx
        return z * nx + x

    barrier = pltpu.get_barrier_semaphore()

    def greet(step, carry):
        pl.semaphore_signal(barrier, inc=1, device_id={"ctx": peer(step)}, device_id_type=MESH)
        return carry

    lax.fori_loop(0, blocks - 1, greet, 0)
    for other in (partner, up, down):
        pl.semaphore_signal(barrier, inc=1, device_id={"ch": other}, device_id_type=MESH)

    loads = [
        pltpu.make_async_copy(src, dst, lsem.at[i])
        for i, (src, dst) in enumerate(
            ((f_hbm, fb), (k_hbm, kb), (v_hbm, vb), (ahead_hbm, ahead), (q_hbm, qb))
        )
    ]
    for load in loads:
        load.start()

    def w_cols(yy, cc):
        return w_hbm.at[:, pl.ds(pl.multiple_of((2 * yy + cc) * cols, cols), cols)]

    w_loads = [
        pltpu.make_async_copy(w_cols(yy, core), wx.at[yy, core], wl_sem.at[yy])
        for yy in range(chips)
    ]
    for load in w_loads:
        load.start()

    lane = lax.broadcasted_iota(jnp.int32, (own, channels), 1) % own
    same = lane == lax.broadcasted_iota(jnp.int32, (own, channels), 0)

    def build(i, carry):
        at = pl.ds(pl.multiple_of(i * own, own), own)
        at_im = pl.ds(pl.multiple_of(channels + i * own, own), own)

        def spread(which):
            row = jnp.broadcast_to(wide_ref[which, pl.ds(i, 1), :], (own, channels))
            return jnp.where(same, row, 0.0).astype(BF16)

        kron_f[at, :] = spread(0)
        kron_f[at_im, :] = spread(1)
        kron_i[at, :channels] = spread(2)
        kron_i[at, channels:] = spread(3)
        tcos[at, :] = jnp.broadcast_to(turn_ref[0, pl.ds(i, 1), :], (own, rows))
        tsin[at, :] = jnp.broadcast_to(turn_ref[1, pl.ds(i, 1), :], (own, rows))
        return carry

    lax.fori_loop(0, blocks, build, 0)

    def slab_copy(send, recv, ssem, rsem, target):
        return pltpu.make_async_remote_copy(
            src_ref=send.at[target], dst_ref=recv.at[me],
            send_sem=ssem.at[target], recv_sem=rsem.at[me],
            device_id={"ctx": target}, device_id_type=MESH,
        )

    def send_all(send, recv, ssem, rsem):
        def one(step, carry):
            slab_copy(send, recv, ssem, rsem, peer(step)).start()
            return carry

        lax.fori_loop(0, blocks - 1, one, 0)

    def take_all(send, recv, ssem, rsem):
        def one(step, carry):
            source = (me + step) % blocks
            pltpu.make_async_remote_copy(
                src_ref=send.at[source], dst_ref=recv.at[source],
                send_sem=ssem.at[source], recv_sem=rsem.at[source],
                device_id={"ctx": source}, device_id_type=MESH,
            ).wait_recv()
            return carry

        lax.fori_loop(1, blocks, one, 0)

    def drain(send, recv, ssem, rsem):
        def one(step, carry):
            slab_copy(send, recv, ssem, rsem, peer(step)).wait_send()
            return carry

        lax.fori_loop(0, blocks - 1, one, 0)

    loads[0].wait()
    send_f[...] = fb[...].T.reshape(blocks, own, rows)
    pl.semaphore_wait(barrier, blocks - 1 + 3)
    send_all(send_f, recv_f, fs_sem, fr_sem)
    loads[1].wait()
    loads[2].wait()
    gated[...] = (kb[...].astype(F32) * vb[...].astype(F32)).astype(BF16)
    send_g[...] = gated[...].T.reshape(blocks, own, rows)
    send_all(send_g, recv_g, gs_sem, gr_sem)
    w_sends = [
        pltpu.make_async_remote_copy(
            src_ref=w_cols(yy, 1 - core), dst_ref=wx.at[yy, core],
            send_sem=ws_sem.at[yy], recv_sem=wr_sem.at[yy],
            device_id={"ch": partner}, device_id_type=MESH,
        )
        for yy in range(chips)
    ]
    for copy in w_sends:
        copy.start()
    recv_f[me] = send_f[me]
    recv_g[me] = send_g[me]
    loads[3].wait()
    loads[4].wait()

    def transform(recv):
        both = dot(kron_f[...], recv[...].reshape(channels, rows))
        re, im = both[:channels], both[channels:]
        turned = jnp.concatenate(
            [re * tcos[...] + im * tsin[...], im * tcos[...] - re * tsin[...]], axis=1
        ).astype(BF16)
        return dot(turned, ahead[...])

    take_all(send_f, recv_f, fs_sem, fr_sem)
    spec[...] = transform(recv_f)
    take_all(send_g, recv_g, gs_sem, gr_sem)
    got = transform(recv_g)
    gr, gi = got[:, :rows], got[:, rows:]
    fr, fi = spec[:, :rows], spec[:, rows:]
    product = jnp.concatenate([gr * fr - gi * fi, gr * fi + gi * fr], axis=1).astype(BF16)
    back = lax.dot_general(
        product, ahead[...], (((1,), (1,)), ((), ())), preferred_element_type=F32
    )
    br, bi = back[:, :rows], back[:, rows:]
    wound[:channels, :] = (br * tcos[...] - bi * tsin[...]).astype(BF16)
    wound[channels:, :] = (bi * tcos[...] + br * tsin[...]).astype(BF16)
    for r in range(PARTS):
        done = dot(kron_i[...], wound[:, r * part:(r + 1) * part]) * (1.0 / (blocks * rows))
        send_y[r] = done.astype(BF16).reshape(blocks, own, part)
        send_all(send_y.at[r], recv_y.at[r], ys_sem.at[r], yr_sem.at[r])
        recv_y[r, me] = send_y[r, me]

    for load in w_loads:
        load.wait()
    for copy in w_sends:
        copy.wait()

    half = part // 2

    def towards(r, way, src, dst, ssem, rsem):
        return pltpu.make_async_remote_copy(
            src_ref=src, dst_ref=dst, send_sem=ssem, recv_sem=rsem,
            device_id={"ch": (up, down)[way]}, device_id_type=MESH,
        )

    def far_copy(r, way):
        return towards(r, way, send_a.at[r, way], recv_a.at[r, way], as_sem.at[r, way], ar_sem.at[r, way])

    def near_copy(r, way, h):
        return towards(
            r, way, send_n.at[r, way, h], recv_n.at[r, way, h], ns_sem.at[r, way, h], nr_sem.at[r, way, h]
        )

    def hid_copy(r):
        return pltpu.make_async_remote_copy(
            src_ref=hid.at[core, r], dst_ref=hid.at[core, r],
            send_sem=hs_sem.at[r], recv_sem=hr_sem.at[r],
            device_id={"ch": partner}, device_id_type=MESH,
        )

    def relay(r):
        far_copy(r, 0).wait_recv()
        send_n[r, 0, 0] = (p_up[r] + recv_a[r, 0].astype(F32)).astype(BF16)
        near_copy(r, 0, 0).start()
        far_copy(r, 1).wait_recv()
        send_n[r, 1, 1] = (p_down[r] + recv_a[r, 1].astype(F32)).astype(BF16)
        near_copy(r, 1, 1).start()

    for r in range(PARTS):
        take_all(send_y.at[r], recv_y.at[r], ys_sem.at[r], yr_sem.at[r])
        conv = recv_y[r].reshape(channels, part).astype(F32).T
        at = slice(r * part, (r + 1) * part)
        mixed = conv + skip_ref[...] * gated[at, :].astype(F32)
        hid[core, r] = (qb[at, :].astype(F32) * mixed).astype(BF16)
        hid_copy(r).start()
        hid_copy(r).wait_recv()

        def terms(yy):
            return dot(hid[0, r], wx[yy, 0]) + dot(hid[1, r], wx[yy, 1])

        far = terms(y_far).astype(BF16)
        send_a[r, 0] = far[:half]
        far_copy(r, 0).start()
        send_a[r, 1] = far[half:]
        far_copy(r, 1).start()
        over = terms(y_up)
        send_n[r, 0, 1] = over[half:].astype(BF16)
        near_copy(r, 0, 1).start()
        p_up[r] = over[:half]
        under = terms(y_down)
        send_n[r, 1, 0] = under[:half].astype(BF16)
        near_copy(r, 1, 0).start()
        p_down[r] = under[half:]
        p_own[r] = terms(y)
        if r > 0:
            relay(r - 1)
    relay(PARTS - 1)
    for r in range(PARTS):
        for h in range(2):
            near_copy(r, 0, h).wait_recv()
            near_copy(r, 1, h).wait_recv()
            total = (
                p_own[r, h * half:(h + 1) * half]
                + recv_n[r, 0, h].astype(F32)
                + recv_n[r, 1, h].astype(F32)
            )
            out_ref[r * part + h * half:r * part + (h + 1) * half, :] = total.astype(BF16)

    drain(send_f, recv_f, fs_sem, fr_sem)
    drain(send_g, recv_g, gs_sem, gr_sem)
    for r in range(PARTS):
        drain(send_y.at[r], recv_y.at[r], ys_sem.at[r], yr_sem.at[r])
        hid_copy(r).wait_send()
        for way in range(2):
            far_copy(r, way).wait_send()
            for h in range(2):
                near_copy(r, way, h).wait_send()


def local(sizes, gate_q, key_k, value_v, long_filter, skip_gain, out_weight):
    rows, channels = key_k.shape
    blocks, lines = sizes
    own = channels // blocks
    chips = lines // 2
    cols = out_weight.shape[1] // lines
    nx = 4 if blocks % 4 == 0 else 1
    part = rows // PARTS
    wide, turn, ahead = tables(blocks, own, rows)
    vmem, dma = pltpu.VMEM, pltpu.SemaphoreType.DMA
    whole = pl.BlockSpec(memory_space=pltpu.VMEM)
    away = pl.BlockSpec(memory_space=pl.ANY)
    slabs = vmem((blocks, own, rows), BF16)
    return pl.pallas_call(
        functools.partial(kernel, (blocks, nx, own, rows, chips)),
        out_shape=jax.ShapeDtypeStruct((rows, cols), BF16),
        in_specs=[away, away, away, away, whole, away, whole, whole, away],
        out_specs=whole,
        scratch_shapes=[
            *[vmem((rows, channels), BF16)] * 5,
            slabs, slabs, slabs, slabs,
            vmem((2 * rows, 2 * rows), BF16),
            vmem((2 * channels, channels), BF16),
            vmem((channels, 2 * channels), BF16),
            vmem((channels, rows), F32),
            vmem((channels, rows), F32),
            vmem((channels, 2 * rows), F32),
            vmem((2 * channels, rows), BF16),
            vmem((PARTS, blocks, own, part), BF16),
            vmem((PARTS, blocks, own, part), BF16),
            vmem((2, PARTS, part, channels), BF16),
            vmem((chips, 2, channels, cols), BF16),
            vmem((PARTS, part, cols), F32),
            vmem((PARTS, part // 2, cols), F32),
            vmem((PARTS, part // 2, cols), F32),
            vmem((PARTS, 2, part // 2, cols), BF16),
            vmem((PARTS, 2, part // 2, cols), BF16),
            vmem((PARTS, 2, 2, part // 2, cols), BF16),
            vmem((PARTS, 2, 2, part // 2, cols), BF16),
            dma((5,)), dma((chips,)), dma((chips,)), dma((chips,)),
            dma((blocks,)), dma((blocks,)), dma((blocks,)), dma((blocks,)),
            dma((PARTS, blocks)), dma((PARTS, blocks)),
            dma((PARTS,)), dma((PARTS,)),
            dma((PARTS, 2)), dma((PARTS, 2)),
            dma((PARTS, 2, 2)), dma((PARTS, 2, 2)),
        ],
        compiler_params=pltpu.CompilerParams(
            collective_id=0, has_side_effects=True, vmem_limit_bytes=60 << 20
        ),
    )(gate_q, key_k, value_v, long_filter, skip_gain[None, :], out_weight, wide, turn, ahead)


def solution(mesh):
    placed = (
        P("ctx", "ch"),
        P("ctx", "ch"),
        P("ctx", "ch"),
        P("ctx", "ch"),
        P("ch"),
        P("ch", None),
    )
    sizes = (mesh.shape["ctx"], mesh.shape["ch"])
    return jax.shard_map(
        functools.partial(local, sizes), mesh=mesh, in_specs=placed, out_specs=P("ctx", "ch"),
        check_vma=False,
    )
```

time: 128 us -> 72.3 us (0.56); the launches traced: 126 us -> 72.2 us
  waiting for transfers between devices: 72.1 us -> 0 us
  Pallas kernels: 0 us -> 70.4 us
  starting transfers between devices: 22.5 us -> 0 us
  between operations: 13.6 us -> 0.01 us
  matrix products: 10.9 us -> 0 us
  local copies, waits for them, and re-layouts: 5.57 us -> 1.77 us
  other arithmetic: 1.38 us -> 0 us
    pallas_call x0 -> x1, Pallas kernels: none -> 70.4 us  [local(): pl.pallas_call(functools.partial(kernel, (blocks, nx, own, rows, chips)),...]
    all_to_all x3 -> x0, waiting for transfers between devices: 37.5 us -> none  [the longest x2 25.2 us: exchange(): lax.all_to_all(value.reshape(blocks, own, rows), 'ctx', split_axis=0, con...]
    reduce_scatter x1 -> x0, waiting for transfers between devices: 34.6 us -> none  [local(): lax.psum_scatter(terms.astype(jnp.bfloat16), 'ch', scatter_dimension=1, t...]
    all_to_all x3 -> x0, starting transfers between devices: 22.5 us -> none  [the longest x2 16.9 us: exchange(): lax.all_to_all(value.reshape(blocks, own, rows), 'ctx', split_axis=0, con...]
    dot_general x10 -> x0, matrix products: 10.9 us -> none  [the longest x1 5.91 us: local(): terms = jnp.dot(hidden, out_weight, preferred_element_type=jnp.float32)]
    unnamed x20 -> x1, local copies, waits for them, and re-layouts: 4.69 us -> 1.77 us
  transfers between devices with their start and end apart: 4 -> 0, of which waited for: 4 -> 0; matrix products, arithmetic and copies ran while one was open for 1% -> 0% of each run, Pallas kernels for 0% -> 0%
where the time goes in v2:
time: 72.3 us; the launch traced here: 72.2 us
  Pallas kernels  70.4 us (97%)
  local copies, waits for them, and re-layouts  1.77 us (2%)
    pallas_call x1, Pallas kernels, local(): pl.pallas_call(functools.partial(kernel, (blocks, nx, own, rows, chips)),...  70.4 us
    unnamed x1, local copies, waits for them, and re-layouts  1.77 us

profile of v2, /device:TPU:1, one launch (start us, length us, event | category | flops | bytes accessed | tf_op | source)
XLA Modules:
  0.0 72.2 jit_solution(18235112046889204389)
XLA Ops:
  0.0 70.4 %shard_map.91 = bf16[384,512]{1,0:T(8,128)(2,1)} custom-call(bf16[384,512]{1,0:T(8,128)(2,1)} %q_hbm.1, bf16[384,512]{1,0:T(8,128)(2,1)} %k_hbm.1, bf16[384,512]{1,0:T(8,128)(2,1)} %v_hbm.1, bf16[384,512]{1,0:T(8,128)(2,1)} %f_hbm.1, f32[1,512]{1,0:T(1,128)} %bitcast.1, bf16[512,4096]{1,0:T(8,128)(2,1)} %w_hbm.1, f32[4,32,512]{2,1,0:T(8,128)} %constant.6.clone.wide_ref, ...), custom_call_target="tpu_custom_call" | custom-call | tf_op jit(solution)/shard_map/pallas_call | solution.py:306
  70.4 1.8 %copy.11 = bf16[384,512]{1,0:T(8,128)(2,1)} copy(bf16[384,512]{1,0:T(8,128)(2,1)} %shard_map.91) | data formatting | bytes 786432

commit v3 on v2

--- a/solution.py
+++ b/solution.py
@@ -37,17 +37,16 @@
     return jnp.dot(a, b, preferred_element_type=F32)
 
 
-def far_first(step, count):
-    half = (step + 1) // 2
-    return (count // 2 + half * (1 - 2 * (step % 2))) % count
+def far_first(count):
+    return [(count // 2 + (i + 1) // 2 * (1 - 2 * (i % 2))) % count for i in range(count)]
 
 
 def kernel(
     dims,
-    q_hbm, k_hbm, v_hbm, f_hbm, skip_ref, w_hbm, wide_ref, turn_ref, ahead_hbm,
+    q_hbm, k_hbm, v_hbm, f_hbm, skip_hbm, w_hbm, wide_hbm, turn_hbm, ahead_hbm,
     out_ref,
-    qb, kb, vb, fb, gated, send_f, send_g, recv_f, recv_g, ahead, kron_f, kron_i, tcos, tsin,
-    spec, wound, send_y, recv_y, hid, wx, p_own, p_up, p_down, send_a, recv_a, send_n, recv_n,
+    skip_ref, wide_ref, turn_ref, qb, kb, vb, fb, gated, send_f, send_g, recv_f, recv_g, ahead, kron_f, kron_i, tcos, tsin,
+    spec, wound, send_y, recv_y, hid, wx, first, p_own, p_up, p_down, send_a, recv_a, send_n, recv_n,
     lsem, wl_sem, ws_sem, wr_sem, fs_sem, fr_sem, gs_sem, gr_sem, ys_sem, yr_sem,
     hs_sem, hr_sem, as_sem, ar_sem, ns_sem, nr_sem,
 ):
@@ -64,25 +63,23 @@
     y_up, y_far, y_down = (y + 1) % chips, (y + 2) % chips, (y + 3) % chips
     up, down = y_up * 2 + core, y_down * 2 + core
 
-    def peer(step):
-        z = (mz + far_first(step // nx, nz)) % nz
-        x = (mx + far_first(step % nx, nx)) % nx
-        return z * nx + x
+    zs = [lax.rem(mz + dz, nz) * nx for dz in range(nz)]
+    xs = [lax.rem(mx + dx, nx) for dx in range(nx)]
+    peers = [zs[dz] + xs[dx] for dz in far_first(nz) for dx in far_first(nx)][:-1]
 
     barrier = pltpu.get_barrier_semaphore()
-
-    def greet(step, carry):
-        pl.semaphore_signal(barrier, inc=1, device_id={"ctx": peer(step)}, device_id_type=MESH)
-        return carry
-
-    lax.fori_loop(0, blocks - 1, greet, 0)
+    for target in peers:
+        pl.semaphore_signal(barrier, inc=1, device_id={"ctx": target}, device_id_type=MESH)
     for other in (partner, up, down):
         pl.semaphore_signal(barrier, inc=1, device_id={"ch": other}, device_id_type=MESH)
 
     loads = [
         pltpu.make_async_copy(src, dst, lsem.at[i])
         for i, (src, dst) in enumerate(
-            ((f_hbm, fb), (k_hbm, kb), (v_hbm, vb), (ahead_hbm, ahead), (q_hbm, qb))
+            (
+                (wide_hbm, wide_ref), (turn_hbm, turn_ref), (f_hbm, fb), (k_hbm, kb),
+                (v_hbm, vb), (ahead_hbm, ahead), (q_hbm, qb), (skip_hbm, skip_ref),
+            )
         )
     ]
     for load in loads:
@@ -98,6 +95,8 @@
     for load in w_loads:
         load.start()
 
+    loads[0].wait()
+    loads[1].wait()
     lane = lax.broadcasted_iota(jnp.int32, (own, channels), 1) % own
     same = lane == lax.broadcasted_iota(jnp.int32, (own, channels), 0)
 
@@ -119,45 +118,27 @@
 
     lax.fori_loop(0, blocks, build, 0)
 
-    def slab_copy(send, recv, ssem, rsem, target):
-        return pltpu.make_async_remote_copy(
-            src_ref=send.at[target], dst_ref=recv.at[me],
-            send_sem=ssem.at[target], recv_sem=rsem.at[me],
-            device_id={"ctx": target}, device_id_type=MESH,
-        )
-
     def send_all(send, recv, ssem, rsem):
-        def one(step, carry):
-            slab_copy(send, recv, ssem, rsem, peer(step)).start()
-            return carry
-
-        lax.fori_loop(0, blocks - 1, one, 0)
-
-    def take_all(send, recv, ssem, rsem):
-        def one(step, carry):
-            source = (me + step) % blocks
+        for target in peers:
             pltpu.make_async_remote_copy(
-                src_ref=send.at[source], dst_ref=recv.at[source],
-                send_sem=ssem.at[source], recv_sem=rsem.at[source],
-                device_id={"ctx": source}, device_id_type=MESH,
-            ).wait_recv()
-            return carry
-
-        lax.fori_loop(1, blocks, one, 0)
-
-    def drain(send, recv, ssem, rsem):
-        def one(step, carry):
-            slab_copy(send, recv, ssem, rsem, peer(step)).wait_send()
-            return carry
-
-        lax.fori_loop(0, blocks - 1, one, 0)
-
-    loads[0].wait()
+                src_ref=send.at[target], dst_ref=recv.at[me], send_sem=ssem, recv_sem=rsem,
+                device_id={"ctx": target}, device_id_type=MESH,
+            ).start()
+        pltpu.make_async_copy(send.at[me], recv.at[me], rsem).start()
+
+    def take_all(recv, rsem):
+        pltpu.make_async_copy(recv, recv, rsem).wait()
+
+    def drain(send, ssem):
+        sent = send.at[pl.ds(0, blocks - 1)]
+        pltpu.make_async_copy(sent, sent, ssem).wait()
+
+    loads[2].wait()
     send_f[...] = fb[...].T.reshape(blocks, own, rows)
     pl.semaphore_wait(barrier, blocks - 1 + 3)
     send_all(send_f, recv_f, fs_sem, fr_sem)
-    loads[1].wait()
-    loads[2].wait()
+    loads[3].wait()
+    loads[4].wait()
     gated[...] = (kb[...].astype(F32) * vb[...].astype(F32)).astype(BF16)
     send_g[...] = gated[...].T.reshape(blocks, own, rows)
     send_all(send_g, recv_g, gs_sem, gr_sem)
@@ -171,10 +152,8 @@
     ]
     for copy in w_sends:
         copy.start()
-    recv_f[me] = send_f[me]
-    recv_g[me] = send_g[me]
-    loads[3].wait()
-    loads[4].wait()
+    for load in loads[5:]:
+        load.wait()
 
     def transform(recv):
         both = dot(kron_f[...], recv[...].reshape(channels, rows))
@@ -184,9 +163,9 @@
         ).astype(BF16)
         return dot(turned, ahead[...])
 
-    take_all(send_f, recv_f, fs_sem, fr_sem)
+    take_all(recv_f, fr_sem)
     spec[...] = transform(recv_f)
-    take_all(send_g, recv_g, gs_sem, gr_sem)
+    take_all(recv_g, gr_sem)
     got = transform(recv_g)
     gr, gi = got[:, :rows], got[:, rows:]
     fr, fi = spec[:, :rows], spec[:, rows:]
@@ -201,7 +180,7 @@
         done = dot(kron_i[...], wound[:, r * part:(r + 1) * part]) * (1.0 / (blocks * rows))
         send_y[r] = done.astype(BF16).reshape(blocks, own, part)
         send_all(send_y.at[r], recv_y.at[r], ys_sem.at[r], yr_sem.at[r])
-        recv_y[r, me] = send_y[r, me]
+
 
     for load in w_loads:
         load.wait()
@@ -240,31 +219,34 @@
         near_copy(r, 1, 1).start()
 
     for r in range(PARTS):
-        take_all(send_y.at[r], recv_y.at[r], ys_sem.at[r], yr_sem.at[r])
+        take_all(recv_y.at[r], yr_sem.at[r])
         conv = recv_y[r].reshape(channels, part).astype(F32).T
         at = slice(r * part, (r + 1) * part)
         mixed = conv + skip_ref[...] * gated[at, :].astype(F32)
         hid[core, r] = (qb[at, :].astype(F32) * mixed).astype(BF16)
         hid_copy(r).start()
+        order = (y_far, y_up, y_down, y)
+        for i, yy in enumerate(order):
+            first[i] = dot(hid[core, r], wx[yy, core])
         hid_copy(r).wait_recv()
 
-        def terms(yy):
-            return dot(hid[0, r], wx[yy, 0]) + dot(hid[1, r], wx[yy, 1])
-
-        far = terms(y_far).astype(BF16)
+        def terms(i):
+            return first[i] + dot(hid[1 - core, r], wx[order[i], 1 - core])
+
+        far = terms(0).astype(BF16)
         send_a[r, 0] = far[:half]
         far_copy(r, 0).start()
         send_a[r, 1] = far[half:]
         far_copy(r, 1).start()
-        over = terms(y_up)
+        over = terms(1)
         send_n[r, 0, 1] = over[half:].astype(BF16)
         near_copy(r, 0, 1).start()
         p_up[r] = over[:half]
-        under = terms(y_down)
+        under = terms(2)
         send_n[r, 1, 0] = under[:half].astype(BF16)
         near_copy(r, 1, 0).start()
         p_down[r] = under[half:]
-        p_own[r] = terms(y)
+        p_own[r] = terms(3)
         if r > 0:
             relay(r - 1)
     relay(PARTS - 1)
@@ -277,12 +259,12 @@
                 + recv_n[r, 0, h].astype(F32)
                 + recv_n[r, 1, h].astype(F32)
             )
-            out_ref[r * part + h * half:r * part + (h + 1) * half, :] = total.astype(BF16)
-
-    drain(send_f, recv_f, fs_sem, fr_sem)
-    drain(send_g, recv_g, gs_sem, gr_sem)
+            out_ref[r * part + h * half:r * part + (h + 1) * half, :] = total
+
+    drain(send_f, fs_sem)
+    drain(send_g, gs_sem)
     for r in range(PARTS):
-        drain(send_y.at[r], recv_y.at[r], ys_sem.at[r], yr_sem.at[r])
+        drain(send_y.at[r], ys_sem.at[r])
         hid_copy(r).wait_send()
         for way in range(2):
             far_copy(r, way).wait_send()
@@ -305,10 +287,11 @@
     slabs = vmem((blocks, own, rows), BF16)
     return pl.pallas_call(
         functools.partial(kernel, (blocks, nx, own, rows, chips)),
-        out_shape=jax.ShapeDtypeStruct((rows, cols), BF16),
-        in_specs=[away, away, away, away, whole, away, whole, whole, away],
+        out_shape=jax.ShapeDtypeStruct((rows, cols), F32),
+        in_specs=[away] * 9,
         out_specs=whole,
         scratch_shapes=[
+            vmem((1, channels), F32), vmem((4, blocks, channels), F32), vmem((2, blocks, rows), F32),
             *[vmem((rows, channels), BF16)] * 5,
             slabs, slabs, slabs, slabs,
             vmem((2 * rows, 2 * rows), BF16),
@@ -322,6 +305,7 @@
             vmem((PARTS, blocks, own, part), BF16),
             vmem((2, PARTS, part, channels), BF16),
             vmem((chips, 2, channels, cols), BF16),
+            vmem((4, part, cols), F32),
             vmem((PARTS, part, cols), F32),
             vmem((PARTS, part // 2, cols), F32),
             vmem((PARTS, part // 2, cols), F32),
@@ -329,9 +313,9 @@
             vmem((PARTS, 2, part // 2, cols), BF16),
             vmem((PARTS, 2, 2, part // 2, cols), BF16),
             vmem((PARTS, 2, 2, part // 2, cols), BF16),
-            dma((5,)), dma((chips,)), dma((chips,)), dma((chips,)),
-            dma((blocks,)), dma((blocks,)), dma((blocks,)), dma((blocks,)),
-            dma((PARTS, blocks)), dma((PARTS, blocks)),
+            dma((8,)), dma((chips,)), dma((chips,)), dma((chips,)),
+            dma, dma, dma, dma,
+            dma((PARTS,)), dma((PARTS,)),
             dma((PARTS,)), dma((PARTS,)),
             dma((PARTS, 2)), dma((PARTS, 2)),
             dma((PARTS, 2, 2)), dma((PARTS, 2, 2)),
@@ -339,7 +323,7 @@
         compiler_params=pltpu.CompilerParams(
             collective_id=0, has_side_effects=True, vmem_limit_bytes=60 << 20
         ),
-    )(gate_q, key_k, value_v, long_filter, skip_gain[None, :], out_weight, wide, turn, ahead)
+    )(gate_q, key_k, value_v, long_filter, skip_gain[None, :], out_weight, wide, turn, ahead).astype(BF16)
 
 
 def solution(mesh):

time: 72.3 us -> 61.9 us (0.86)
  Pallas kernels: 70.4 us -> 59.9 us
  other arithmetic: 0 us -> 1.93 us
  local copies, waits for them, and re-layouts: 1.77 us -> 0 us
    pallas_call x1, Pallas kernels: 70.4 us -> 59.9 us  [local(): pl.pallas_call(functools.partial(kernel, (blocks, nx, own, rows, chips)),...]
    convert_element_type x0 -> x1, other arithmetic: none -> 1.93 us  [local(): return pl.pallas_call(functools.partial(kernel, (blocks, nx, own, rows, c...]
    unnamed x1 -> x0, local copies, waits for them, and re-layouts: 1.77 us -> none
where the time goes in v3:
time: 61.9 us; the launch traced here: 61.8 us
  Pallas kernels  59.9 us (97%)
  other arithmetic  1.93 us (3%)
    pallas_call x1, Pallas kernels, local(): pl.pallas_call(functools.partial(kernel, (blocks, nx, own, rows, chips)),...  59.9 us
    convert_element_type x1, other arithmetic, local(): return pl.pallas_call(functools.partial(kernel, (blocks, nx, own, rows, c...  1.93 us

profile of v3, /device:TPU:1, one launch (start us, length us, event | category | flops | bytes accessed | tf_op | source)
XLA Modules:
  0.0 61.8 jit_solution(11170740512461467510)
XLA Ops:
  0.0 59.9 %shard_map.91 = f32[384,512]{1,0:T(8,128)} custom-call(bf16[384,512]{1,0:T(8,128)(2,1)} %q_hbm.1, bf16[384,512]{1,0:T(8,128)(2,1)} %k_hbm.1, bf16[384,512]{1,0:T(8,128)(2,1)} %v_hbm.1, bf16[384,512]{1,0:T(8,128)(2,1)} %f_hbm.1, f32[1,512]{1,0:T(1,128)} %bitcast.1, bf16[512,4096]{1,0:T(8,128)(2,1)} %w_hbm.1, f32[4,32,512]{2,1,0:T(8,128)} %constant.6.clone.wide_hbm, ...), custom_call_target="tpu_custom_call" | custom-call | tf_op jit(solution)/shard_map/pallas_call | solution.py:288
  59.9 1.9 %convert_element_type.3 = bf16[384,512]{1,0:T(8,128)(2,1)} convert(f32[384,512]{1,0:T(8,128)} %shard_map.91) | non-fusion elementwise | flops 196608 | bytes 1179648 | tf_op jit(solution)/shard_map/convert_element_type | solution.py:326

commit v4 on v3

--- a/solution.py
+++ b/solution.py
@@ -46,11 +46,13 @@
     q_hbm, k_hbm, v_hbm, f_hbm, skip_hbm, w_hbm, wide_hbm, turn_hbm, ahead_hbm,
     out_ref,
     skip_ref, wide_ref, turn_ref, qb, kb, vb, fb, gated, send_f, send_g, recv_f, recv_g, ahead, kron_f, kron_i, tcos, tsin,
-    spec, wound, send_y, recv_y, hid, wx, first, p_own, p_up, p_down, send_a, recv_a, send_n, recv_n,
-    lsem, wl_sem, ws_sem, wr_sem, fs_sem, fr_sem, gs_sem, gr_sem, ys_sem, yr_sem,
+    spec, wound, send_a_half, recv_a_half, send_y, recv_y, hid, wx, first, p_own, p_up, p_down, send_a, recv_a, send_n, recv_n,
+    lsem, wl_sem, ws_sem, wr_sem, fs_sem, fr_sem, gs_sem, gr_sem, as_half, ar_half, ys_sem, yr_sem,
     hs_sem, hr_sem, as_sem, ar_sem, ns_sem, nr_sem,
 ):
     blocks, nx, own, rows, chips = dims
+    few = own // 2
+    lot = blocks * few
     nz = blocks // nx
     channels = blocks * own
     part = rows // PARTS
@@ -97,26 +99,31 @@
 
     loads[0].wait()
     loads[1].wait()
-    lane = lax.broadcasted_iota(jnp.int32, (own, channels), 1) % own
-    same = lane == lax.broadcasted_iota(jnp.int32, (own, channels), 0)
+    lane = lax.broadcasted_iota(jnp.int32, (own, lot), 1) % few
+    same = lane == lax.broadcasted_iota(jnp.int32, (own, lot), 0) % few
 
     def build(i, carry):
         at = pl.ds(pl.multiple_of(i * own, own), own)
-        at_im = pl.ds(pl.multiple_of(channels + i * own, own), own)
+        at_im = pl.ds(pl.multiple_of(lot + i * own, own), own)
+
+        def pair(table, which, width):
+            return jnp.concatenate(
+                [jnp.broadcast_to(table[which, pl.ds(2 * i + j, 1), :], (few, width)) for j in range(2)],
+                axis=0,
+            )
 
         def spread(which):
-            row = jnp.broadcast_to(wide_ref[which, pl.ds(i, 1), :], (own, channels))
-            return jnp.where(same, row, 0.0).astype(BF16)
+            return jnp.where(same, pair(wide_ref, which, lot), 0.0).astype(BF16)
 
         kron_f[at, :] = spread(0)
         kron_f[at_im, :] = spread(1)
-        kron_i[at, :channels] = spread(2)
-        kron_i[at, channels:] = spread(3)
-        tcos[at, :] = jnp.broadcast_to(turn_ref[0, pl.ds(i, 1), :], (own, rows))
-        tsin[at, :] = jnp.broadcast_to(turn_ref[1, pl.ds(i, 1), :], (own, rows))
+        kron_i[at, :lot] = spread(2)
+        kron_i[at, lot:] = spread(3)
+        tcos[at, :] = pair(turn_ref, 0, rows)
+        tsin[at, :] = pair(turn_ref, 1, rows)
         return carry
 
-    lax.fori_loop(0, blocks, build, 0)
+    lax.fori_loop(0, blocks // 2, build, 0)
 
     def send_all(send, recv, ssem, rsem):
         for target in peers:
@@ -134,14 +141,17 @@
         pltpu.make_async_copy(sent, sent, ssem).wait()
 
     loads[2].wait()
-    send_f[...] = fb[...].T.reshape(blocks, own, rows)
+    send_f[...] = fb[...].astype(F32).T.reshape(blocks, 2, few, rows).astype(BF16)
     pl.semaphore_wait(barrier, blocks - 1 + 3)
     send_all(send_f, recv_f, fs_sem, fr_sem)
     loads[3].wait()
     loads[4].wait()
-    gated[...] = (kb[...].astype(F32) * vb[...].astype(F32)).astype(BF16)
-    send_g[...] = gated[...].T.reshape(blocks, own, rows)
-    send_all(send_g, recv_g, gs_sem, gr_sem)
+    rounded = (kb[...].astype(F32) * vb[...].astype(F32)).astype(BF16)
+    gated[...] = rounded
+    turned_g = rounded.astype(F32).T.reshape(blocks, 2, few, rows)
+    for h in range(2):
+        send_g[h] = turned_g[:, h].astype(BF16)
+        send_all(send_g.at[h], recv_g.at[h], gs_sem.at[h], gr_sem.at[h])
     w_sends = [
         pltpu.make_async_remote_copy(
             src_ref=w_cols(yy, 1 - core), dst_ref=wx.at[yy, core],
@@ -155,32 +165,42 @@
     for load in loads[5:]:
         load.wait()
 
-    def transform(recv):
-        both = dot(kron_f[...], recv[...].reshape(channels, rows))
-        re, im = both[:channels], both[channels:]
+    def transform(slabs):
+        both = dot(kron_f[...], slabs.astype(F32).reshape(lot, rows).astype(BF16))
+        re, im = both[:lot], both[lot:]
         turned = jnp.concatenate(
             [re * tcos[...] + im * tsin[...], im * tcos[...] - re * tsin[...]], axis=1
         ).astype(BF16)
         return dot(turned, ahead[...])
 
+    def convolve(h):
+        got = transform(recv_g[h])
+        gr, gi = got[:, :rows], got[:, rows:]
+        fr, fi = spec[h, :, :rows], spec[h, :, rows:]
+        product = jnp.concatenate([gr * fr - gi * fi, gr * fi + gi * fr], axis=1).astype(BF16)
+        back = lax.dot_general(
+            product, ahead[...], (((1,), (1,)), ((), ())), preferred_element_type=F32
+        )
+        br, bi = back[:, :rows], back[:, rows:]
+        wound[h, :lot, :] = (br * tcos[...] - bi * tsin[...]).astype(BF16)
+        wound[h, lot:, :] = (bi * tcos[...] + br * tsin[...]).astype(BF16)
+
+    def finish(h, at, width):
+        done = dot(kron_i[...], wound[h, :, at]) * (1.0 / (blocks * rows))
+        return done.reshape(blocks, few, width).astype(BF16)
+
     take_all(recv_f, fr_sem)
-    spec[...] = transform(recv_f)
-    take_all(recv_g, gr_sem)
-    got = transform(recv_g)
-    gr, gi = got[:, :rows], got[:, rows:]
-    fr, fi = spec[:, :rows], spec[:, rows:]
-    product = jnp.concatenate([gr * fr - gi * fi, gr * fi + gi * fr], axis=1).astype(BF16)
-    back = lax.dot_general(
-        product, ahead[...], (((1,), (1,)), ((), ())), preferred_element_type=F32
-    )
-    br, bi = back[:, :rows], back[:, rows:]
-    wound[:channels, :] = (br * tcos[...] - bi * tsin[...]).astype(BF16)
-    wound[channels:, :] = (bi * tcos[...] + br * tsin[...]).astype(BF16)
+    for h in range(2):
+        spec[h] = transform(recv_f[:, h])
+    take_all(recv_g.at[0], gr_sem.at[0])
+    convolve(0)
+    send_a_half[...] = finish(0, slice(0, rows), rows)
+    send_all(send_a_half, recv_a_half, as_half, ar_half)
+    take_all(recv_g.at[1], gr_sem.at[1])
+    convolve(1)
     for r in range(PARTS):
-        done = dot(kron_i[...], wound[:, r * part:(r + 1) * part]) * (1.0 / (blocks * rows))
-        send_y[r] = done.astype(BF16).reshape(blocks, own, part)
+        send_y[r] = finish(1, slice(r * part, (r + 1) * part), part)
         send_all(send_y.at[r], recv_y.at[r], ys_sem.at[r], yr_sem.at[r])
-
 
     for load in w_loads:
         load.wait()
@@ -218,10 +238,12 @@
         send_n[r, 1, 1] = (p_down[r] + recv_a[r, 1].astype(F32)).astype(BF16)
         near_copy(r, 1, 1).start()
 
+    take_all(recv_a_half, ar_half)
     for r in range(PARTS):
+        at = slice(r * part, (r + 1) * part)
         take_all(recv_y.at[r], yr_sem.at[r])
-        conv = recv_y[r].reshape(channels, part).astype(F32).T
-        at = slice(r * part, (r + 1) * part)
+        halves = [recv_a_half[:, :, at].astype(F32), recv_y[r].astype(F32)]
+        conv = jnp.stack(halves, axis=1).reshape(channels, part).T
         mixed = conv + skip_ref[...] * gated[at, :].astype(F32)
         hid[core, r] = (qb[at, :].astype(F32) * mixed).astype(BF16)
         hid_copy(r).start()
@@ -262,7 +284,9 @@
             out_ref[r * part + h * half:r * part + (h + 1) * half, :] = total
 
     drain(send_f, fs_sem)
-    drain(send_g, gs_sem)
+    for h in range(2):
+        drain(send_g.at[h], gs_sem.at[h])
+    drain(send_a_half, as_half)
     for r in range(PARTS):
         drain(send_y.at[r], ys_sem.at[r])
         hid_copy(r).wait_send()
@@ -280,29 +304,34 @@
     cols = out_weight.shape[1] // lines
     nx = 4 if blocks % 4 == 0 else 1
     part = rows // PARTS
-    wide, turn, ahead = tables(blocks, own, rows)
+    few = own // 2
+    lot = blocks * few
+    wide, turn, ahead = tables(blocks, few, rows)
     vmem, dma = pltpu.VMEM, pltpu.SemaphoreType.DMA
     whole = pl.BlockSpec(memory_space=pltpu.VMEM)
     away = pl.BlockSpec(memory_space=pl.ANY)
-    slabs = vmem((blocks, own, rows), BF16)
+    slabs = vmem((blocks, 2, few, rows), BF16)
+    split = vmem((2, blocks, few, rows), BF16)
     return pl.pallas_call(
         functools.partial(kernel, (blocks, nx, own, rows, chips)),
-        out_shape=jax.ShapeDtypeStruct((rows, cols), F32),
+        out_shape=pltpu.VMEM((rows, cols), F32),
         in_specs=[away] * 9,
         out_specs=whole,
         scratch_shapes=[
-            vmem((1, channels), F32), vmem((4, blocks, channels), F32), vmem((2, blocks, rows), F32),
+            vmem((1, channels), F32), vmem(wide.shape, F32), vmem((2, blocks, rows), F32),
             *[vmem((rows, channels), BF16)] * 5,
-            slabs, slabs, slabs, slabs,
+            slabs, split, slabs, split,
             vmem((2 * rows, 2 * rows), BF16),
-            vmem((2 * channels, channels), BF16),
-            vmem((channels, 2 * channels), BF16),
-            vmem((channels, rows), F32),
-            vmem((channels, rows), F32),
-            vmem((channels, 2 * rows), F32),
-            vmem((2 * channels, rows), BF16),
-            vmem((PARTS, blocks, own, part), BF16),
-            vmem((PARTS, blocks, own, part), BF16),
+            vmem((2 * lot, lot), BF16),
+            vmem((lot, 2 * lot), BF16),
+            vmem((lot, rows), F32),
+            vmem((lot, rows), F32),
+            vmem((2, lot, 2 * rows), F32),
+            vmem((2, 2 * lot, rows), BF16),
+            vmem((blocks, few, rows), BF16),
+            vmem((blocks, few, rows), BF16),
+            vmem((PARTS, blocks, few, part), BF16),
+            vmem((PARTS, blocks, few, part), BF16),
             vmem((2, PARTS, part, channels), BF16),
             vmem((chips, 2, channels, cols), BF16),
             vmem((4, part, cols), F32),
@@ -314,7 +343,7 @@
             vmem((PARTS, 2, 2, part // 2, cols), BF16),
             vmem((PARTS, 2, 2, part // 2, cols), BF16),
             dma((8,)), dma((chips,)), dma((chips,)), dma((chips,)),
-            dma, dma, dma, dma,
+            dma, dma, dma((2,)), dma((2,)), dma, dma,
             dma((PARTS,)), dma((PARTS,)),
             dma((PARTS,)), dma((PARTS,)),
             dma((PARTS, 2)), dma((PARTS, 2)),

time: 61.9 us -> 58.1 us (0.939)
  Pallas kernels: 59.9 us -> 57.2 us
  other arithmetic: 1.93 us -> 0.8 us
    pallas_call x1, Pallas kernels: 59.9 us -> 57.2 us  [local(): pl.pallas_call(functools.partial(kernel, (blocks, nx, own, rows, chips)),...]
    convert_element_type x1, other arithmetic: 1.93 us -> 0.8 us  [local(): return pl.pallas_call(functools.partial(kernel, (blocks, nx, own, rows, c...]
where the time goes in v4:
time: 58.1 us; the launch traced here: 58 us
  Pallas kernels  57.2 us (98%)
  other arithmetic  0.8 us (1%)
    pallas_call x1, Pallas kernels, local(): pl.pallas_call(functools.partial(kernel, (blocks, nx, own, rows, chips)),...  57.2 us

profile of v4, /device:TPU:1, one launch (start us, length us, event | category | flops | bytes accessed | tf_op | source)
XLA Modules:
  0.0 58.0 jit_solution(17609296349169477890)
XLA Ops:
  0.0 57.2 %shard_map.91 = f32[384,512]{1,0:T(8,128)S(1)} custom-call(bf16[384,512]{1,0:T(8,128)(2,1)} %q_hbm.1, bf16[384,512]{1,0:T(8,128)(2,1)} %k_hbm.1, bf16[384,512]{1,0:T(8,128)(2,1)} %v_hbm.1, bf16[384,512]{1,0:T(8,128)(2,1)} %f_hbm.1, f32[1,512]{1,0:T(1,128)} %bitcast.1, bf16[512,4096]{1,0:T(8,128)(2,1)} %w_hbm.1, f32[4,32,256]{2,1,0:T(8,128)} %constant.6.clone.wide_hbm, ...), custom_call_target="tpu_custom_call" | custom-call | tf_op jit(solution)/shard_map/pallas_call | solution.py:315
  57.2 0.8 %convert_element_type.3 = bf16[384,512]{1,0:T(8,128)(2,1)} convert(f32[384,512]{1,0:T(8,128)S(1)} %shard_map.91) | non-fusion elementwise | flops 196608 | bytes 1179648 | tf_op jit(solution)/shard_map/convert_element_type | solution.py:355

commit v5 on v4

--- a/solution.py
+++ b/solution.py
@@ -46,9 +46,9 @@
     q_hbm, k_hbm, v_hbm, f_hbm, skip_hbm, w_hbm, wide_hbm, turn_hbm, ahead_hbm,
     out_ref,
     skip_ref, wide_ref, turn_ref, qb, kb, vb, fb, gated, send_f, send_g, recv_f, recv_g, ahead, kron_f, kron_i, tcos, tsin,
-    spec, wound, send_a_half, recv_a_half, send_y, recv_y, hid, wx, first, p_own, p_up, p_down, send_a, recv_a, send_n, recv_n,
-    lsem, wl_sem, ws_sem, wr_sem, fs_sem, fr_sem, gs_sem, gr_sem, as_half, ar_half, ys_sem, yr_sem,
-    hs_sem, hr_sem, as_sem, ar_sem, ns_sem, nr_sem,
+    spec, wound, send_a_half, recv_a_half, send_a_end, recv_a_end, send_y, recv_y, early, hid, wx, first, p_own, p_up, p_down, send_a, recv_a, send_n, recv_n,
+    lsem, wl_sem, ws_sem, wr_sem, fs_sem, fr_sem, gs_sem, gr_sem, as_half, ar_half, as_end, ar_end, ys_sem, yr_sem,
+    es_sem, er_sem, hs_sem, hr_sem, as_sem, ar_sem, ns_sem, nr_sem,
 ):
     blocks, nx, own, rows, chips = dims
     few = own // 2
@@ -141,16 +141,18 @@
         pltpu.make_async_copy(sent, sent, ssem).wait()
 
     loads[2].wait()
-    send_f[...] = fb[...].astype(F32).T.reshape(blocks, 2, few, rows).astype(BF16)
+    turned_f = fb[...].astype(F32).T.reshape(2, blocks, few, rows)
+    for h in range(2):
+        send_f[:, h] = turned_f[h].astype(BF16)
     pl.semaphore_wait(barrier, blocks - 1 + 3)
     send_all(send_f, recv_f, fs_sem, fr_sem)
     loads[3].wait()
     loads[4].wait()
     rounded = (kb[...].astype(F32) * vb[...].astype(F32)).astype(BF16)
     gated[...] = rounded
-    turned_g = rounded.astype(F32).T.reshape(blocks, 2, few, rows)
+    turned_g = rounded.astype(F32).T.reshape(2, blocks, few, rows)
     for h in range(2):
-        send_g[h] = turned_g[:, h].astype(BF16)
+        send_g[h] = turned_g[h].astype(BF16)
         send_all(send_g.at[h], recv_g.at[h], gs_sem.at[h], gr_sem.at[h])
     w_sends = [
         pltpu.make_async_remote_copy(
@@ -173,34 +175,43 @@
         ).astype(BF16)
         return dot(turned, ahead[...])
 
-    def convolve(h):
+    def multiply(h):
         got = transform(recv_g[h])
         gr, gi = got[:, :rows], got[:, rows:]
         fr, fi = spec[h, :, :rows], spec[h, :, rows:]
-        product = jnp.concatenate([gr * fr - gi * fi, gr * fi + gi * fr], axis=1).astype(BF16)
-        back = lax.dot_general(
-            product, ahead[...], (((1,), (1,)), ((), ())), preferred_element_type=F32
-        )
-        br, bi = back[:, :rows], back[:, rows:]
-        wound[h, :lot, :] = (br * tcos[...] - bi * tsin[...]).astype(BF16)
-        wound[h, lot:, :] = (bi * tcos[...] + br * tsin[...]).astype(BF16)
-
-    def finish(h, at, width):
-        done = dot(kron_i[...], wound[h, :, at]) * (1.0 / (blocks * rows))
-        return done.reshape(blocks, few, width).astype(BF16)
-
+        return jnp.concatenate([gr * fr - gi * fi, gr * fi + gi * fr], axis=1).astype(BF16)
+
+    def finish(product, first_row, last_row):
+        at = slice(first_row, last_row)
+
+        def back(kind):
+            return lax.dot_general(
+                product, ahead[kind * rows + first_row:kind * rows + last_row, :],
+                (((1,), (1,)), ((), ())), preferred_element_type=F32,
+            )
+
+        br, bi = back(0), back(1)
+        wound[:lot, at] = (br * tcos[:, at] - bi * tsin[:, at]).astype(BF16)
+        wound[lot:, at] = (bi * tcos[:, at] + br * tsin[:, at]).astype(BF16)
+        done = dot(kron_i[...], wound[:, at]) * (1.0 / (blocks * rows))
+        return done.reshape(blocks, few, last_row - first_row).astype(BF16)
+
+    last = rows - part
     take_all(recv_f, fr_sem)
     for h in range(2):
         spec[h] = transform(recv_f[:, h])
     take_all(recv_g.at[0], gr_sem.at[0])
-    convolve(0)
-    send_a_half[...] = finish(0, slice(0, rows), rows)
+    product = multiply(0)
+    send_a_half[...] = finish(product, 0, last)
     send_all(send_a_half, recv_a_half, as_half, ar_half)
+    send_a_end[...] = finish(product, last, rows)
     take_all(recv_g.at[1], gr_sem.at[1])
-    convolve(1)
+    product = multiply(1)
     for r in range(PARTS):
-        send_y[r] = finish(1, slice(r * part, (r + 1) * part), part)
+        send_y[r] = finish(product, r * part, (r + 1) * part)
         send_all(send_y.at[r], recv_y.at[r], ys_sem.at[r], yr_sem.at[r])
+        if r == 0:
+            send_all(send_a_end, recv_a_end, as_end, ar_end)
 
     for load in w_loads:
         load.wait()
@@ -229,6 +240,23 @@
             send_sem=hs_sem.at[r], recv_sem=hr_sem.at[r],
             device_id={"ch": partner}, device_id_type=MESH,
         )
+
+    spans = (pl.ds(0, last), pl.ds(last, part))
+
+    def early_copy(e):
+        view = early.at[core, spans[e]]
+        return pltpu.make_async_remote_copy(
+            src_ref=view, dst_ref=view, send_sem=es_sem.at[e], recv_sem=er_sem.at[e],
+            device_id={"ch": partner}, device_id_type=MESH,
+        )
+
+    order = (y_far, y_up, y_down, y)
+
+    def gate(slabs, at, h):
+        over = slice(h * lot, (h + 1) * lot)
+        conv = slabs.astype(F32).reshape(lot, slabs.shape[2]).T
+        mixed = conv + skip_ref[:, over] * gated[at, over].astype(F32)
+        return (qb[at, over].astype(F32) * mixed).astype(BF16)
 
     def relay(r):
         far_copy(r, 0).wait_recv()
@@ -238,22 +266,33 @@
         send_n[r, 1, 1] = (p_down[r] + recv_a[r, 1].astype(F32)).astype(BF16)
         near_copy(r, 1, 1).start()
 
-    take_all(recv_a_half, ar_half)
-    for r in range(PARTS):
+    def early_begin(e, slabs):
+        at = (slice(0, last), slice(last, rows))[e]
+        early[core, at] = gate(slabs[...], at, 0)
+        early_copy(e).start()
+        for i, yy in enumerate(order):
+            first[i, at] = dot(early[core, at], wx[yy, core, :lot])
+
+    def early_end(e):
+        at = (slice(0, last), slice(last, rows))[e]
+        early_copy(e).wait_recv()
+        for i, yy in enumerate(order):
+            first[i, at] += dot(early[1 - core, at], wx[yy, 1 - core, :lot])
+
+    def begin(r):
         at = slice(r * part, (r + 1) * part)
         take_all(recv_y.at[r], yr_sem.at[r])
-        halves = [recv_a_half[:, :, at].astype(F32), recv_y[r].astype(F32)]
-        conv = jnp.stack(halves, axis=1).reshape(channels, part).T
-        mixed = conv + skip_ref[...] * gated[at, :].astype(F32)
-        hid[core, r] = (qb[at, :].astype(F32) * mixed).astype(BF16)
+        hid[core, r] = gate(recv_y[r], at, 1)
         hid_copy(r).start()
-        order = (y_far, y_up, y_down, y)
         for i, yy in enumerate(order):
-            first[i] = dot(hid[core, r], wx[yy, core])
+            first[i, at] += dot(hid[core, r], wx[yy, core, lot:])
+
+    def emit(r):
+        at = slice(r * part, (r + 1) * part)
         hid_copy(r).wait_recv()
 
         def terms(i):
-            return first[i] + dot(hid[1 - core, r], wx[order[i], 1 - core])
+            return first[i, at] + dot(hid[1 - core, r], wx[order[i], 1 - core, lot:])
 
         far = terms(0).astype(BF16)
         send_a[r, 0] = far[:half]
@@ -269,9 +308,22 @@
         near_copy(r, 1, 0).start()
         p_down[r] = under[half:]
         p_own[r] = terms(3)
-        if r > 0:
-            relay(r - 1)
-    relay(PARTS - 1)
+
+    take_all(recv_a_half, ar_half)
+    early_begin(0, recv_a_half)
+    early_end(0)
+    begin(0)
+    begin(1)
+    emit(0)
+    take_all(recv_a_end, ar_end)
+    early_begin(1, recv_a_end)
+    emit(1)
+    early_end(1)
+    begin(2)
+    relay(0)
+    emit(2)
+    relay(1)
+    relay(2)
     for r in range(PARTS):
         for h in range(2):
             near_copy(r, 0, h).wait_recv()
@@ -287,9 +339,13 @@
     for h in range(2):
         drain(send_g.at[h], gs_sem.at[h])
     drain(send_a_half, as_half)
+    drain(send_a_end, as_end)
     for r in range(PARTS):
         drain(send_y.at[r], ys_sem.at[r])
         hid_copy(r).wait_send()
+        if r == 0:
+            early_copy(0).wait_send()
+            early_copy(1).wait_send()
         for way in range(2):
             far_copy(r, way).wait_send()
             for h in range(2):
@@ -327,14 +383,15 @@
             vmem((lot, rows), F32),
             vmem((lot, rows), F32),
             vmem((2, lot, 2 * rows), F32),
-            vmem((2, 2 * lot, rows), BF16),
-            vmem((blocks, few, rows), BF16),
-            vmem((blocks, few, rows), BF16),
+            vmem((2 * lot, rows), BF16),
+            *[vmem((blocks, few, rows - part), BF16)] * 2,
+            *[vmem((blocks, few, part), BF16)] * 2,
             vmem((PARTS, blocks, few, part), BF16),
             vmem((PARTS, blocks, few, part), BF16),
-            vmem((2, PARTS, part, channels), BF16),
+            vmem((2, rows, lot), BF16),
+            vmem((2, PARTS, part, lot), BF16),
             vmem((chips, 2, channels, cols), BF16),
-            vmem((4, part, cols), F32),
+            vmem((4, rows, cols), F32),
             vmem((PARTS, part, cols), F32),
             vmem((PARTS, part // 2, cols), F32),
             vmem((PARTS, part // 2, cols), F32),
@@ -343,9 +400,9 @@
             vmem((PARTS, 2, 2, part // 2, cols), BF16),
             vmem((PARTS, 2, 2, part // 2, cols), BF16),
             dma((8,)), dma((chips,)), dma((chips,)), dma((chips,)),
-            dma, dma, dma((2,)), dma((2,)), dma, dma,
+            dma, dma, dma((2,)), dma((2,)), dma, dma, dma, dma,
             dma((PARTS,)), dma((PARTS,)),
-            dma((PARTS,)), dma((PARTS,)),
+            dma((2,)), dma((2,)), dma((PARTS,)), dma((PARTS,)),
             dma((PARTS, 2)), dma((PARTS, 2)),
             dma((PARTS, 2, 2)), dma((PARTS, 2, 2)),
         ],

time: 58.1 us -> 57 us (0.981)
  Pallas kernels: 57.2 us -> 56.1 us
    pallas_call x1, Pallas kernels: 57.2 us -> 56.1 us  [local(): pl.pallas_call(functools.partial(kernel, (blocks, nx, own, rows, chips)),...]
where the time goes in v5:
time: 57 us; the launch traced here: 56.9 us
  Pallas kernels  56.1 us (98%)
  other arithmetic  0.8 us (1%)
    pallas_call x1, Pallas kernels, local(): pl.pallas_call(functools.partial(kernel, (blocks, nx, own, rows, chips)),...  56.1 us

profile of v5, /device:TPU:1, one launch (start us, length us, event | category | flops | bytes accessed | tf_op | source)
XLA Modules:
  0.0 56.9 jit_solution(12178246778598076742)
XLA Ops:
  0.0 56.1 %shard_map.91 = f32[384,512]{1,0:T(8,128)S(1)} custom-call(bf16[384,512]{1,0:T(8,128)(2,1)} %q_hbm.1, bf16[384,512]{1,0:T(8,128)(2,1)} %k_hbm.1, bf16[384,512]{1,0:T(8,128)(2,1)} %v_hbm.1, bf16[384,512]{1,0:T(8,128)(2,1)} %f_hbm.1, f32[1,512]{1,0:T(1,128)} %bitcast.1, bf16[512,4096]{1,0:T(8,128)(2,1)} %w_hbm.1, f32[4,32,256]{2,1,0:T(8,128)} %constant.6.clone.wide_hbm, ...), custom_call_target="tpu_custom_call" | custom-call | tf_op jit(solution)/shard_map/pallas_call | solution.py:371
  56.1 0.8 %convert_element_type.3 = bf16[384,512]{1,0:T(8,128)(2,1)} convert(f32[384,512]{1,0:T(8,128)S(1)} %shard_map.91) | non-fusion elementwise | flops 196608 | bytes 1179648 | tf_op jit(solution)/shard_map/convert_element_type | solution.py:412
